TPU v7x, 512 devices: a whole 4x8x8 slice. The times are simulated.
512 devices in a mesh: al: 16 (over z_lo, x), row: 32 (over y, z_hi, core).
Axes of the slice: x: 4, y: 8, z: 8 (z_hi: 2, z_lo: 4; z = z_hi * 4 + z_lo), core: 2. Of those that a mesh axis runs over, the one named last changes fastest.
Arguments:
- psi: float32 [16, 2, 1024, 16, 512], P('al', None, 'row'), may hold values from -6 to 6
- angular: int32 [16, 16], replicated, may hold values from 0 to 15, each once within a row
- widths: int32 [32], P('row'), may hold values from 2 to 5
- field: float32 [1], replicated, may hold values from 0.2 to 0.6
- elem_matrix: bfloat16 [32, 32], replicated, may hold values from -1 to 1
- outer_matrix: bfloat16 [512, 512], replicated, may hold values from -1 to 1
Outputs:
- advanced: float32 [16, 2, 1024, 16, 512], P('al', None, 'row')
Inputs may be any that keep to these rules, and one draw needn't show every extreme that they name: `angular`: each row holds every value 0 to 15 once.
All inputs are finite; a program needn't handle non-finite values.
Results may differ from a plain program's by a relative error of at most 0.0013.
Values sent between devices are 32-bit elements; how exact they have to be, the bound alone decides.
A program may use at most 128 MiB of HBM per device.

v0:
```python
import jax
import jax.numpy as jnp
from jax import lax
from jax.sharding import PartitionSpec as P

P_SIZE = 32
L2 = 16
R2 = 512
ORDER = 4


dt_step = 0.35
radius_zero = 8.0
radial_step = 0.25
dipole_scale = 64.0


def entering(value, axis, join, neutral):
    count, mine = (lax.axis_size(axis), lax.axis_index(axis))
    pieces = lax.all_gather(value, axis)
    running = jnp.full_like(value, 0) + jnp.asarray(neutral, value.dtype)

    def step(position, running):
        longer = join(running, pieces[position])
        return jnp.where(position < mine, longer, running)

    return lax.fori_loop(0, count - 1, step, running)


def extended(value, sides, width):
    for axis, dim in sides:
        size, length = (lax.axis_size(axis), value.shape[dim])
        up = [(i, (i + 1) % size) for i in range(size - 1)]
        down = [(j, i) for i, j in up]
        last = lax.slice_in_dim(value, length - width, length, axis=dim)
        first = lax.slice_in_dim(value, 0, width, axis=dim)
        before = lax.ppermute(last, axis, up)
        after = lax.ppermute(first, axis, down)
        value = jnp.concatenate([before, value, after], axis=dim)
    return value


def coupling_weight(level):
    return (level + 1.0) / jnp.sqrt((2.0 * level + 1.0) * (2.0 * level + 3.0))


def add_ints(earlier, later):
    return earlier + later


def local(psi, angular, widths, field, elem_matrix, outer_matrix):
    level_count = psi.shape[0]
    slab_points = psi.shape[2]
    elem_count = widths.shape[0]
    plane = L2 * R2
    offset = entering(jnp.sum(widths), "row", add_ints, jnp.int32(0))
    edges = (offset + jnp.cumsum(widths) - widths).astype(jnp.float32)
    nodes = jnp.arange(P_SIZE).astype(jnp.float32) / (P_SIZE - 1)
    wide = widths.astype(jnp.float32)
    radius_one = (radius_zero + edges[:, None] + wide[:, None] * nodes[None, :]).reshape(-1)
    scales = 4.0 / (wide * wide)
    row_scales = jnp.repeat(scales, P_SIZE)
    block_elem = jnp.kron(jnp.eye(elem_count, dtype=jnp.bfloat16), elem_matrix)
    radius_two = radius_zero + radial_step * jnp.arange(R2).astype(jnp.float32)
    row_index = lax.axis_index("row")
    row_final = lax.axis_size("row") - 1
    base = lax.axis_index("al") * level_count
    level_total = lax.axis_size("al") * level_count
    level_ids = base + jnp.arange(level_count, dtype=jnp.int32)
    levels = level_ids.astype(jnp.float32)
    blank_row = -jnp.ones((1, angular.shape[1]), jnp.int32)
    padded_perm = jnp.concatenate([blank_row, angular, blank_row], 0)
    window = lax.dynamic_slice_in_dim(padded_perm, base, level_count + 2, 0)
    own_perm = window[1:-1]
    below_perm = window[:-2]
    above_perm = window[2:]
    values = own_perm.astype(jnp.float32)
    cent_one = (
        levels[:, None] * (levels[:, None] + 1.0) / (2.0 * radius_one[None, :] ** 2)
        - 2.0 / radius_one[None, :]
    )
    cent_two = (
        values[:, :, None] * (values[:, :, None] + 1.0) / (2.0 * radius_two[None, None, :] ** 2)
        - 2.0 / radius_two[None, None, :]
    )
    repulsion = 1.0 / jnp.maximum(radius_one[:, None], radius_two[None, :])
    match_below = (own_perm[:, :, None] == below_perm[:, None, :]).astype(jnp.float32)
    match_above = (own_perm[:, :, None] == above_perm[:, None, :]).astype(jnp.float32)
    weight_below = coupling_weight(jnp.maximum(levels - 1.0, 0.0)) * (level_ids > 0).astype(
        jnp.float32
    )
    weight_above = coupling_weight(levels) * (level_ids < level_total - 1).astype(jnp.float32)
    first_rows = jnp.arange(elem_count, dtype=jnp.int32) * P_SIZE
    last_rows = first_rows + (P_SIZE - 1)

    def potential():
        total = cent_one[:, :, None, None] + cent_two[:, None, :, :] + repulsion[None, :, None, :]
        return total.reshape(level_count, slab_points, plane)

    def raw_image(state):
        rounded = state.astype(jnp.bfloat16)
        inner = jnp.stack([jnp.dot(block_elem, rounded[0], preferred_element_type=jnp.float32)], 0)
        outer = jnp.dot(rounded.reshape(-1, R2), outer_matrix, preferred_element_type=jnp.float32)
        return inner * row_scales[None, :, None] + outer.reshape(state.shape) + potential() * state

    def apply_ham(parts):
        totals = [raw_image(part) for part in parts]
        firsts = [total[:, 0::P_SIZE] for total in totals]
        lasts = [total[:, P_SIZE - 1 :: P_SIZE] for total in totals]
        rims = jnp.stack([jnp.stack([firsts[k][:, 0], lasts[k][:, -1]], 1) for k in range(2)], 1)
        beside = extended(rims, (("row", 2),), 1)
        images = []
        for k in range(2):
            head = jnp.where(row_index == 0, 0.0, firsts[k][:, 0] + beside[:, k, 0])
            tail = jnp.where(row_index == row_final, 0.0, lasts[k][:, -1] + beside[:, k, 3])
            joined = firsts[k][:, 1:] + lasts[k][:, :-1]
            new_first = jnp.concatenate([head[:, None], joined], 1)
            new_last = jnp.concatenate([joined, tail[:, None]], 1)
            fixed = totals[k].at[:, first_rows].set(new_first).at[:, last_rows].set(new_last)
            images.append(fixed)
        return images

    strength = field[0]
    real_part = psi[:, 0].reshape(level_count, slab_points, plane)
    imag_part = psi[:, 1].reshape(level_count, slab_points, plane)
    finish = ORDER + 1
    term = (real_part, imag_part)
    accum = (real_part, imag_part)
    for power in range(1, finish):
        image = apply_ham(term)
        factor = dt_step / power
        term = (factor * image[1], -factor * image[0])
        accum = (accum[0] + term[0], accum[1] + term[1])
    padded = extended(psi, (("al", 0),), 1)
    below = padded[:-2]
    above = padded[2:]
    mixed = weight_below[:, None, None, None, None] * jnp.einsum(
        "isq,icnqj->icnsj", match_below, below, precision=lax.Precision.HIGHEST
    )
    mixed = mixed + weight_above[:, None, None, None, None] * jnp.einsum(
        "isq,icnqj->icnsj", match_above, above, precision=lax.Precision.HIGHEST
    )
    reach = (strength * radius_one / dipole_scale)[None, :, None, None]
    grid_shape = (level_count, slab_points, L2, R2)
    psi = jnp.stack(
        [
            accum[0].reshape(grid_shape) + reach * mixed[:, 1],
            accum[1].reshape(grid_shape) - reach * mixed[:, 0],
        ],
        1,
    )
    return psi


def solution(mesh):
    placed = (P("al", None, "row", None, None), P(), P("row"), P(), P(), P())
    return jax.shard_map(
        local,
        mesh=mesh,
        in_specs=placed,
        out_specs=P("al", None, "row", None, None),
        check_vma=False,
    )
```

profile of v0, /device:TPU:89, one launch (start us, length us, event | category | flops | bytes accessed | tf_op | source)
XLA Modules:
  0.0 255.2 jit_solution(15904127157236481500)
XLA Ops:
  1.9 3.3 %fusion.82 = (bf16[1,1,32,16,512]{4,3,2,1,0:T(8,128)(2,1)S(1)}, bf16[1,1,32,16,512]{4,3,2,1,0:T(8,128)(2,1)}) fusion(f32[1,2,32,16,512]{4,3,2,1,0:T(8,128)} %param.40), kind=kLoop, calls=%fused_computation.172 | loop fusion | bytes 2097152 | tf_op jit(solution)/shard_map/slice | solution.py:124
  7.9 19.6 %all-reduce = s32[32]{0:T(128)S(1)} all-reduce(s32[32]{0:T(128)S(1)} %dynamic-update-slice.48), channel_id=1, replica_groups=mesh['al'=16,'row'=32] {'row'}, use_global_device_ids=true, to_apply=%add | all-reduce | flops 32 | bytes 256
  27.5 42.0 %while.29 = (s32[]{:T(128)}, s32[]{:T(128)}, s32[]{:T(128)}, s32[32]{0:T(128)S(1)}, s32[]{:T(128)}) while((s32[]{:T(128)}, s32[]{:T(128)}, s32[]{:T(128)}, s32[32]{0:T(128)S(1)}, s32[]{:T(128)}) %tuple.128), condition=%wide.region_1.2_spmd, body=%wide.region_0.0_spmd.sunk | while | flops 5 | bytes 107 | solution.py:27
  75.2 2.5 reshape.1110
  87.9 10.2 %collective-permute-start = (f32[1,2,1,8192]{3,2,1,0:T(1,128)S(1)}, f32[1,2,1,8192]{3,2,1,0:T(1,128)S(1)}, u32[]{:S(2)}, u32[]{:S(2)}) collective-permute-start(f32[1,2,1,8192]{3,2,1,0:T(1,128)S(1)} %get-tuple-element.340), channel_id=1, source_target_pairs={{0,1},{1,2},{2,3},{3,4},{4,5},{5,6},{6,7},{7,8},{8,9},{9,10},{10,1... | collective-permute-start | bytes 196616 | tf_op jit(solution)/shard_map/ppermute | solution.py:37
  101.5 6.4 %collective-permute-done.1 = f32[1,2,1,8192]{3,2,1,0:T(1,128)S(1)} collective-permute-done((f32[1,2,1,8192]{3,2,1,0:T(1,128)S(1)}, f32[1,2,1,8192]{3,2,1,0:T(1,128)S(1)}, u32[]{:S(2)}, u32[]{:S(2)}) %collective-permute-start.1) | collective-permute-done | bytes 65568 | tf_op jit(solution)/shard_map/ppermute | solution.py:38
  117.7 2.5 fusion.25
  126.3 2.4 fusion.93
  128.7 2.4 reshape.1113
  131.1 2.2 fusion.24
  135.6 2.6 %collective-permute-start.3 = (f32[1,2,1,8192]{3,2,1,0:T(1,128)S(1)}, f32[1,2,1,8192]{3,2,1,0:T(1,128)S(1)}, u32[]{:S(2)}, u32[]{:S(2)}) collective-permute-start(f32[1,2,1,8192]{3,2,1,0:T(1,128)S(1)} %get-tuple-element.337), channel_id=1, source_target_pairs={{1,0},{2,1},{3,2},{4,3},{5,4},{6,5},{7,6},{8,7},{9,8},{10,9},{11,1... | collective-permute-start | bytes 196616 | tf_op jit(solution)/shard_map/ppermute | solution.py:38
  138.2 6.9 %collective-permute-done.3 = f32[1,2,1,8192]{3,2,1,0:T(1,128)S(1)} collective-permute-done((f32[1,2,1,8192]{3,2,1,0:T(1,128)S(1)}, f32[1,2,1,8192]{3,2,1,0:T(1,128)S(1)}, u32[]{:S(2)}, u32[]{:S(2)}) %collective-permute-start.3) | collective-permute-done | bytes 65568 | tf_op jit(solution)/shard_map/ppermute | solution.py:38
  152.0 2.2 fusion.27
  160.2 2.4 fusion.95
  162.7 2.4 reshape.1117
  165.1 2.3 fusion.26
  169.7 2.4 collective-permute-start.5
  172.1 3.1 %collective-permute-start.8 = (f32[1,2,32,16,512]{4,3,2,1,0:T(8,128)}, f32[1,2,32,16,512]{4,3,2,1,0:T(8,128)}, u32[]{:S(2)}, u32[]{:S(2)}) collective-permute-start(f32[1,2,32,16,512]{4,3,2,1,0:T(8,128)} %param.40), channel_id=1, source_target_pairs={{0,32},{32,64},{64,96},{96,128},{128,160},{160,192},{192,224},{224... | collective-permute-start | bytes 6291464 | tf_op jit(solution)/shard_map/ppermute | solution.py:37
  175.2 4.3 %collective-permute-start.9 = (f32[1,2,32,16,512]{4,3,2,1,0:T(8,128)}, f32[1,2,32,16,512]{4,3,2,1,0:T(8,128)}, u32[]{:S(2)}, u32[]{:S(2)}) collective-permute-start(f32[1,2,32,16,512]{4,3,2,1,0:T(8,128)} %param.40), channel_id=1, source_target_pairs={{32,0},{64,32},{96,64},{128,96},{160,128},{192,160},{224,192},{256... | collective-permute-start | bytes 6291464 | tf_op jit(solution)/shard_map/ppermute | solution.py:38
  185.6 2.4 fusion.98
  188.0 2.4 reshape.1123
  190.4 2.2 fusion.29
  195.1 2.4 fusion.97
  197.5 2.4 reshape.1121
  201.9 7.6 %collective-permute-start.6 = (f32[1,2,1,8192]{3,2,1,0:T(1,128)S(1)}, f32[1,2,1,8192]{3,2,1,0:T(1,128)S(1)}, u32[]{:S(2)}, u32[]{:S(2)}) collective-permute-start(f32[1,2,1,8192]{3,2,1,0:T(1,128)S(1)} %get-tuple-element.334), channel_id=1, source_target_pairs={{0,1},{1,2},{2,3},{3,4},{4,5},{5,6},{6,7},{7,8},{8,9},{9,10},{10,1... | collective-permute-start | bytes 196616 | tf_op jit(solution)/shard_map/ppermute | solution.py:37
  211.7 2.5 reshape_squeeze.13
  214.2 2.4 reshape_squeeze.10
  216.7 9.0 %collective-permute-done.6 = f32[1,2,1,8192]{3,2,1,0:T(1,128)S(1)} collective-permute-done((f32[1,2,1,8192]{3,2,1,0:T(1,128)S(1)}, f32[1,2,1,8192]{3,2,1,0:T(1,128)S(1)}, u32[]{:S(2)}, u32[]{:S(2)}) %collective-permute-start.6) | collective-permute-done | bytes 65568 | tf_op jit(solution)/shard_map/ppermute | solution.py:37
  225.7 6.9 %collective-permute-done.7 = f32[1,2,1,8192]{3,2,1,0:T(1,128)S(1)} collective-permute-done((f32[1,2,1,8192]{3,2,1,0:T(1,128)S(1)}, f32[1,2,1,8192]{3,2,1,0:T(1,128)S(1)}, u32[]{:S(2)}, u32[]{:S(2)}) %collective-permute-start.7) | collective-permute-done | bytes 65568 | tf_op jit(solution)/shard_map/ppermute | solution.py:38
  244.9 2.2 multiply_add_fusion.1
  247.7 2.7 %fusion.32 = f32[16,2,32,512]{3,0,2,1:T(8,128)S(1)} fusion(f32[1,2,32,16,512]{4,3,2,1,0:T(8,128)} %collective-permute-done.8, s32[16]{0:T(128)S(1)} %get-tuple-element.343, s32[16]{0:T(128)S(1)} %get-tuple-element.342), kind=kOutput, calls=%fused_computation.41 | convolution fusion | flops 100663552 | bytes 4194432 | tf_op jit(solution)/shard_map/isq,icnqj->icnsj/dot_general | solution.py:137
  250.4 3.1 %add_bitcast_fusion = f32[1,2,32,16,512]{4,3,2,1,0:T(8,128)S(1)} fusion(f32[16,2,32,512]{3,0,2,1:T(8,128)S(1)} %fusion.32, f32[1,2,32,16,512]{4,3,2,1,0:T(8,128)} %collective-permute-done.9, f32[]{:T(128)S(6)} %mul.395, f32[]{:T(128)S(6)} %mul.394, s32[16]{0:T(128)S(1)} %get-tuple-element.341, s32[16]{0:T(128)S(1)} %get-tuple-element.342), kind=kOutput, calls=%fused_computation.43 | convolution fusion | flops 102236416 | bytes 6291592 | tf_op jit(solution)/shard_map/isq,icnqj->icnsj/dot_general | solution.py:140
  (178 shorter events, 102.4 us)
Async XLA Ops:
  0.0 73.8 %copy-start = (bf16[512,512]{1,0:T(8,128)(2,1)S(1)}, bf16[512,512]{1,0:T(8,128)(2,1)}, u32[]{:S(2)}) copy-start(bf16[512,512]{1,0:T(8,128)(2,1)} %param.45) | copy-start | bytes 1572868
  1.8 70.4 %copy-start.11 = (f32[1,1,32,16,512]{4,3,2,1,0:T(8,128)}, f32[1,1,32,16,512]{4,3,2,1,0:T(8,128)S(1)}, u32[]{:S(2)}) copy-start(f32[1,1,32,16,512]{4,3,2,1,0:T(8,128)S(1)} %get-tuple-element.290) | copy-start | bytes 3145732
  1.8 80.3 %copy-start.10 = (f32[1,1,32,16,512]{4,3,2,1,0:T(8,128)}, f32[1,1,32,16,512]{4,3,2,1,0:T(8,128)S(1)}, u32[]{:S(2)}) copy-start(f32[1,1,32,16,512]{4,3,2,1,0:T(8,128)S(1)} %get-tuple-element.289) | copy-start | bytes 3145732
  1.8 68.4 %copy-start.19 = (s32[16,16]{1,0:T(8,128)S(1)}, s32[16,16]{1,0:T(8,128)}, u32[]{:S(2)}) copy-start(s32[16,16]{1,0:T(8,128)} %param.41) | copy-start | bytes 3076
  70.6 3.2 %copy-start.9 = (f32[32,16,512]{2,1,0:T(8,128)}, f32[32,16,512]{2,1,0:T(8,128)S(1)}, u32[]{:S(2)}) copy-start(f32[32,16,512]{2,1,0:T(8,128)S(1)} %add.511) | copy-start | bytes 3145732
  70.6 3.2 %copy-start.16 = (bf16[1,1,32,16,512]{4,3,2,1,0:T(8,128)(2,1)S(1)}, bf16[1,1,32,16,512]{4,3,2,1,0:T(8,128)(2,1)}, u32[]{:S(2)}) copy-start(bf16[1,1,32,16,512]{4,3,2,1,0:T(8,128)(2,1)} %get-tuple-element.292) | copy-start | bytes 1572868
  75.2 4.0 %copy-start.12 = (f32[4,8,16,512]{3,1,2,0:T(8,128)S(1)}, f32[4,8,16,512]{3,1,2,0:T(8,128)}, u32[]{:S(2)}) copy-start(f32[4,8,16,512]{3,1,2,0:T(8,128)} %copy.12) | copy-start | bytes 3145732
  75.2 4.0 %copy-start.18 = (bf16[32,32]{1,0:T(8,128)(2,1)S(1)}, bf16[32,32]{1,0:T(8,128)(2,1)}, u32[]{:S(2)}) copy-start(bf16[32,32]{1,0:T(8,128)(2,1)} %param.44) | copy-start | bytes 6148
  81.1 1.0 copy-start.8
  84.2 1.5 copy-start.13
  87.6 26.4 %copy-start.7 = (f32[1,32,8192]{2,1,0:T(8,128)}, f32[1,32,8192]{2,1,0:T(8,128)S(1)}, u32[]{:S(2)}) copy-start(f32[1,32,8192]{2,1,0:T(8,128)S(1)} %fusion.20) | copy-start | bytes 3145732
  87.9 13.6 %collective-permute-start = (f32[1,2,1,8192]{3,2,1,0:T(1,128)S(1)}, f32[1,2,1,8192]{3,2,1,0:T(1,128)S(1)}, u32[]{:S(2)}, u32[]{:S(2)}) collective-permute-start(f32[1,2,1,8192]{3,2,1,0:T(1,128)S(1)} %get-tuple-element.340), channel_id=1, source_target_pairs={{0,1},{1,2},{2,3},{3,4},{4,5},{5,6},{6,7},{7,8},{8,9},{9,10},{10,1... | collective-permute-start | bytes 196616 | tf_op jit(solution)/shard_map/ppermute | solution.py:37
  98.1 9.8 %collective-permute-start.1 = (f32[1,2,1,8192]{3,2,1,0:T(1,128)S(1)}, f32[1,2,1,8192]{3,2,1,0:T(1,128)S(1)}, u32[]{:S(2)}, u32[]{:S(2)}) collective-permute-start(f32[1,2,1,8192]{3,2,1,0:T(1,128)S(1)} %get-tuple-element.339), channel_id=1, source_target_pairs={{1,0},{2,1},{3,2},{4,3},{5,4},{6,5},{7,6},{8,7},{9,8},{10,9},{11,1... | collective-permute-start | bytes 196616 | tf_op jit(solution)/shard_map/ppermute | solution.py:38
  120.1 25.0 %copy-start.1 = (f32[1,32,8192]{2,1,0:T(8,128)}, f32[1,32,8192]{2,1,0:T(8,128)S(1)}, u32[]{:S(2)}) copy-start(f32[1,32,8192]{2,1,0:T(8,128)S(1)} %fusion.25) | copy-start | bytes 3145732
  133.4 11.9 %copy-start.5 = (f32[1,32,8192]{2,1,0:T(8,128)}, f32[1,32,8192]{2,1,0:T(8,128)S(1)}, u32[]{:S(2)}) copy-start(f32[1,32,8192]{2,1,0:T(8,128)S(1)} %fusion.24) | copy-start | bytes 3145732
  133.7 4.5 %collective-permute-start.2 = (f32[1,2,1,8192]{3,2,1,0:T(1,128)S(1)}, f32[1,2,1,8192]{3,2,1,0:T(1,128)S(1)}, u32[]{:S(2)}, u32[]{:S(2)}) collective-permute-start(f32[1,2,1,8192]{3,2,1,0:T(1,128)S(1)} %get-tuple-element.338), channel_id=1, source_target_pairs={{0,1},{1,2},{2,3},{3,4},{4,5},{5,6},{6,7},{7,8},{8,9},{9,10},{10,1... | collective-permute-start | bytes 196616 | tf_op jit(solution)/shard_map/ppermute | solution.py:37
  135.6 9.5 %collective-permute-start.3 = (f32[1,2,1,8192]{3,2,1,0:T(1,128)S(1)}, f32[1,2,1,8192]{3,2,1,0:T(1,128)S(1)}, u32[]{:S(2)}, u32[]{:S(2)}) collective-permute-start(f32[1,2,1,8192]{3,2,1,0:T(1,128)S(1)} %get-tuple-element.337), channel_id=1, source_target_pairs={{1,0},{2,1},{3,2},{4,3},{5,4},{6,5},{7,6},{8,7},{9,8},{10,9},{11,1... | collective-permute-start | bytes 196616 | tf_op jit(solution)/shard_map/ppermute | solution.py:38
  167.4 12.1 %copy-start.3 = (f32[1,32,8192]{2,1,0:T(8,128)}, f32[1,32,8192]{2,1,0:T(8,128)S(1)}, u32[]{:S(2)}) copy-start(f32[1,32,8192]{2,1,0:T(8,128)S(1)} %fusion.26) | copy-start | bytes 3145732
  167.7 11.8 %collective-permute-start.4 = (f32[1,2,1,8192]{3,2,1,0:T(1,128)S(1)}, f32[1,2,1,8192]{3,2,1,0:T(1,128)S(1)}, u32[]{:S(2)}, u32[]{:S(2)}) collective-permute-start(f32[1,2,1,8192]{3,2,1,0:T(1,128)S(1)} %get-tuple-element.336), channel_id=1, source_target_pairs={{0,1},{1,2},{2,3},{3,4},{4,5},{5,6},{6,7},{7,8},{8,9},{9,10},{10,1... | collective-permute-start | bytes 196616 | tf_op jit(solution)/shard_map/ppermute | solution.py:37
  169.7 9.8 %collective-permute-start.5 = (f32[1,2,1,8192]{3,2,1,0:T(1,128)S(1)}, f32[1,2,1,8192]{3,2,1,0:T(1,128)S(1)}, u32[]{:S(2)}, u32[]{:S(2)}) collective-permute-start(f32[1,2,1,8192]{3,2,1,0:T(1,128)S(1)} %get-tuple-element.335), channel_id=1, source_target_pairs={{1,0},{2,1},{3,2},{4,3},{5,4},{6,5},{7,6},{8,7},{9,8},{10,9},{11,1... | collective-permute-start | bytes 196616 | tf_op jit(solution)/shard_map/ppermute | solution.py:38
  172.1 75.6 %collective-permute-start.8 = (f32[1,2,32,16,512]{4,3,2,1,0:T(8,128)}, f32[1,2,32,16,512]{4,3,2,1,0:T(8,128)}, u32[]{:S(2)}, u32[]{:S(2)}) collective-permute-start(f32[1,2,32,16,512]{4,3,2,1,0:T(8,128)} %param.40), channel_id=1, source_target_pairs={{0,32},{32,64},{64,96},{96,128},{128,160},{160,192},{192,224},{224... | collective-permute-start | bytes 6291464 | tf_op jit(solution)/shard_map/ppermute | solution.py:37
  175.2 75.2 %collective-permute-start.9 = (f32[1,2,32,16,512]{4,3,2,1,0:T(8,128)}, f32[1,2,32,16,512]{4,3,2,1,0:T(8,128)}, u32[]{:S(2)}, u32[]{:S(2)}) collective-permute-start(f32[1,2,32,16,512]{4,3,2,1,0:T(8,128)} %param.40), channel_id=1, source_target_pairs={{32,0},{64,32},{96,64},{128,96},{160,128},{192,160},{224,192},{256... | collective-permute-start | bytes 6291464 | tf_op jit(solution)/shard_map/ppermute | solution.py:38
  192.7 1.0 copy-start.14
  201.5 10.1 %copy-start.15 = (f32[1,32,8192]{2,1,0:T(8,128)}, f32[1,32,8192]{2,1,0:T(8,128)S(1)}, u32[]{:S(2)}) copy-start(f32[1,32,8192]{2,1,0:T(8,128)S(1)} %fusion.28) | copy-start | bytes 3145732
  201.9 23.8 %collective-permute-start.6 = (f32[1,2,1,8192]{3,2,1,0:T(1,128)S(1)}, f32[1,2,1,8192]{3,2,1,0:T(1,128)S(1)}, u32[]{:S(2)}, u32[]{:S(2)}) collective-permute-start(f32[1,2,1,8192]{3,2,1,0:T(1,128)S(1)} %get-tuple-element.334), channel_id=1, source_target_pairs={{0,1},{1,2},{2,3},{3,4},{4,5},{5,6},{6,7},{7,8},{8,9},{9,10},{10,1... | collective-permute-start | bytes 196616 | tf_op jit(solution)/shard_map/ppermute | solution.py:37
  209.5 23.1 %collective-permute-start.7 = (f32[1,2,1,8192]{3,2,1,0:T(1,128)S(1)}, f32[1,2,1,8192]{3,2,1,0:T(1,128)S(1)}, u32[]{:S(2)}, u32[]{:S(2)}) collective-permute-start(f32[1,2,1,8192]{3,2,1,0:T(1,128)S(1)} %get-tuple-element.333), channel_id=1, source_target_pairs={{1,0},{2,1},{3,2},{4,3},{5,4},{6,5},{7,6},{8,7},{9,8},{10,9},{11,1... | collective-permute-start | bytes 196616 | tf_op jit(solution)/shard_map/ppermute | solution.py:38
  211.7 25.8 %copy-start.2 = (f32[1,32,8192]{2,1,0:T(8,128)S(1)}, f32[1,32,8192]{2,1,0:T(8,128)}, u32[]{:S(2)}) copy-start(f32[1,32,8192]{2,1,0:T(8,128)} %scatter.65) | copy-start | bytes 3145732
  239.7 5.2 %copy-start.4 = (f32[1,32,8192]{2,1,0:T(8,128)S(1)}, f32[1,32,8192]{2,1,0:T(8,128)}, u32[]{:S(2)}) copy-start(f32[1,32,8192]{2,1,0:T(8,128)} %scatter.69) | copy-start | bytes 3145732
  239.7 5.2 %copy-start.6 = (f32[1,32,8192]{2,1,0:T(8,128)S(1)}, f32[1,32,8192]{2,1,0:T(8,128)}, u32[]{:S(2)}) copy-start(f32[1,32,8192]{2,1,0:T(8,128)} %scatter.61) | copy-start | bytes 3145732
  250.4 3.1 %copy-start.17 = (f32[4,8,16,512]{3,2,1,0:T(8,128)S(1)}, f32[4,8,16,512]{3,2,1,0:T(8,128)}, u32[]{:S(2)}) copy-start(f32[4,8,16,512]{3,2,1,0:T(8,128)} %copy.17) | copy-start | bytes 3145732
  250.4 3.1 %copy-start.20 = (f32[1,2,32,16,512]{4,3,2,1,0:T(8,128)S(1)}, f32[1,2,32,16,512]{4,3,2,1,0:T(8,128)}, u32[]{:S(2)}) copy-start(f32[1,2,32,16,512]{4,3,2,1,0:T(8,128)} %custom-call) | copy-start | bytes 6291460
  253.9 1.3 copy-start.21
where the time goes:
time: 257 us; the launch traced here: 255 us
  local copies, waits for them, and re-layouts  92.5 us (36%)
  starting transfers between devices  38.2 us (15%)
  matrix products  36.2 us (14%)
  waiting for transfers between devices  29.3 us (11%)
  loops' own time  21.8 us (8%)
  blocking collectives  19.6 us (8%)
  other arithmetic  15.2 us (6%)
    scatter x16, local copies, waits for them, and re-layouts, apply_ham(): totals[k].at[:, first_rows].set(new_first).at[:, last_rows].set(new_last)  25.3 us
    ppermute x5, starting transfers between devices, extended(): before = lax.ppermute(last, axis, up)  24.8 us
    another operation x1, loops' own time, entering(): return lax.fori_loop(0, count - 1, step, running)  21.8 us
    ppermute x5, waiting for transfers between devices, extended(): after = lax.ppermute(first, axis, down)  20.2 us
    dynamic_slice x31, local copies, waits for them, and re-layouts, step(): longer = join(running, pieces[position])  20.2 us
    unnamed x1, blocking collectives  19.6 us
    dot_general x8, matrix products, raw_image(): jnp.dot(block_elem, rounded[0], preferred_element_type=jnp.float32)  16.9 us
    reshape x8, local copies, waits for them, and re-layouts, raw_image(): outer.reshape(state.shape)  15.5 us
  transfers between devices with their start and end apart: 10, of which 4 were waited for; matrix products, arithmetic and copies ran while one was open for 18% of the time, Pallas kernels for 0%

commit v1 on v0

v1 whole, which is shorter than its diff:
```python
import functools

import jax
import jax.numpy as jnp
from jax import lax
from jax.experimental import pallas as pl
from jax.experimental.pallas import tpu as pltpu
from jax.sharding import PartitionSpec as P

MESH = pl.DeviceIdType.MESH
F32 = jnp.float32
BF16 = jnp.bfloat16

P_SIZE = 32
L2 = 16
R2 = 512
ORDER = 4
SUB = 8
GROUPS = L2 // SUB
ROWS = P_SIZE * SUB
QUAD = 4
CHUNKS = 4
CHUNK = P_SIZE // CHUNKS
MIXROWS = CHUNK * L2

dt_step = 0.35
radius_zero = 8.0
radial_step = 0.25
dipole_scale = 64.0


def iota(shape, dim):
    return lax.broadcasted_iota(jnp.int32, shape, dim)


def dot(a, b):
    return jnp.dot(a, b, preferred_element_type=F32)


def dot_lhs_t(a, b):
    return lax.dot_general(a, b, (((0,), (0,)), ((), ())), preferred_element_type=F32)


def ones_where(mask):
    return jnp.where(mask, 1.0, 0.0).astype(BF16)


def spread(size, inner, count):
    rows = iota((size, count), 0)
    rows = rows // inner if inner else rows % count
    return ones_where(rows == iota((size, count), 1))


def spread_t(size, inner, count):
    cols = iota((count, size), 1)
    cols = cols // inner if inner else cols % count
    return ones_where(cols == iota((count, size), 0))


def coupling_weight(level):
    return (level + 1.0) / jnp.sqrt((2.0 * level + 1.0) * (2.0 * level + 3.0))


def kernel(
    al_size, row_size,
    psi, ang, widths, field, elem, outer_hbm,
    out,
    xs, xbs, pot, below, above, outer_m, ke, kp, mix, cent2, potn, reach,
    psi_rim, rim_in, rim_out, op, partial, w_own, w_quad, w_total, w_ys,
    local_sem, bulk_send, bulk_recv, rim_send, rim_recv, psi_send, psi_recv, w_send, w_recv,
):
    a = lax.axis_index("al")
    r = lax.axis_index("row")
    quads = row_size // QUAD
    q = r % QUAD
    y = r // QUAD
    has_al = (a > 0, a < al_size - 1)
    has_row = (r > 0, r < row_size - 1)

    fetch_psi = pltpu.make_async_copy(psi, xs.at[0], local_sem.at[0])
    fetch_acc = pltpu.make_async_copy(psi, out, local_sem.at[1])
    fetch_outer = pltpu.make_async_copy(outer_hbm, outer_m, local_sem.at[2])
    fetch_psi.start()
    fetch_outer.start()
    fetch_acc.start()

    barrier = pltpu.get_barrier_semaphore()
    quad_peers = [y * QUAD + (q + j) % QUAD for j in range(1, QUAD)]
    y_peers = [((y + j) % quads) * QUAD + q for j in range(1, quads)]
    for peer in quad_peers + y_peers:
        pl.semaphore_signal(barrier, inc=1, device_id={"row": peer}, device_id_type=MESH)
    for side in range(2):
        step = 2 * side - 1

        @pl.when(has_al[side])
        def _():
            pl.semaphore_signal(barrier, inc=1, device_id={"al": a + step}, device_id_type=MESH)

        @pl.when(has_row[side])
        def _():
            pl.semaphore_signal(barrier, inc=1, device_id={"row": r + step}, device_id_type=MESH)

    w_own[...] = jnp.full((8, 128), widths[0], jnp.int32)
    wide = jnp.full((8, 128), widths[0], jnp.int32).astype(F32)
    scale = jnp.max(4.0 / (wide * wide))
    ef = elem[...].astype(F32)
    ri, ci = iota((P_SIZE, P_SIZE), 0), iota((P_SIZE, P_SIZE), 1)
    ends = (0, P_SIZE - 1)
    corner = [[jnp.sum(jnp.where((ri == i) & (ci == k), ef, 0.0)) * scale for k in ends] for i in ends]
    wide_rows = dot(spread(ROWS, SUB, P_SIZE), elem[...]).astype(BF16)
    kron = dot(wide_rows, spread_t(ROWS, SUB, P_SIZE))
    kr, kc = iota((ROWS, ROWS), 0), iota((ROWS, ROWS), 1)
    kron = jnp.where(kr % SUB == kc % SUB, kron, 0.0)
    ke[...] = kron.astype(BF16)
    inside = (kc >= SUB) & (kc < ROWS - SUB)
    kron = jnp.where(inside, kron, 0.0)
    kp[...] = jnp.concatenate([kron[0:SUB], kron[ROWS - SUB :]], 0).astype(BF16)

    angf = ang[...]
    slots = iota((L2, L2), 0)

    def one_hot(level):
        row = jnp.sum(jnp.where(slots == level, angf, 0), axis=0, keepdims=True)
        return ones_where(jnp.broadcast_to(row, (L2, L2)) == slots)

    own_hot = one_hot(a)
    mr, mc = iota((MIXROWS, MIXROWS), 0), iota((MIXROWS, MIXROWS), 1)
    for side in range(2):
        level = jnp.clip(a + 2 * side - 1, 0, al_size - 1)
        match = dot_lhs_t(own_hot, one_hot(level)).astype(BF16)
        tall = dot(spread(MIXROWS, 0, L2), match).astype(BF16)
        full = dot(tall, spread_t(MIXROWS, 0, L2))
        mix[side] = jnp.where(mr // L2 == mc // L2, full, 0.0).astype(BF16)
    momenta = iota((L2, R2), 0)
    square = dot_lhs_t(own_hot, (momenta * (momenta + 1)).astype(F32).astype(BF16))
    radius_two = radius_zero + radial_step * iota((L2, R2), 1).astype(F32)
    cent = square / (2.0 * radius_two * radius_two) - 2.0 / radius_two
    cent2[...] = cent.reshape(GROUPS, SUB, R2)

    level_one = jnp.full((8, 128), a, jnp.int32).astype(F32)
    weights = (
        jnp.max(coupling_weight(jnp.maximum(level_one - 1.0, 0.0))),
        jnp.max(coupling_weight(level_one)),
    )
    for side, buf in enumerate((below, above)):

        @pl.when(jnp.logical_not(has_al[side]))
        def _():
            def clear(n, _):
                for part in range(2):
                    buf[part, n] = jnp.zeros((GROUPS, SUB, R2), F32)
                return 0

            lax.fori_loop(0, P_SIZE, clear, 0)

    fetch_psi.wait()
    fetch_outer.wait()

    def partial_sums(slot, block):
        sums = dot(kp[...], xbs[slot, block]) * scale
        partial[0, block] = sums[0:SUB]
        partial[1, block] = sums[SUB:]

    def round_start(block, _):
        c, g = block // GROUPS, block % GROUPS
        xbs[0, block] = xs[0, c, :, g].reshape(ROWS, R2).astype(BF16)
        partial_sums(0, block)
        return 0

    lax.fori_loop(0, 2 * GROUPS, round_start, 0)

    def rim_rounded(slot, c, end):
        return xs[slot, c, ends[end]].astype(BF16).astype(F32)

    def rim_copy(k, side):
        return pltpu.make_async_remote_copy(
            src_ref=rim_out.at[k, side],
            dst_ref=rim_in.at[k, 1 - side],
            send_sem=rim_send.at[k, side],
            recv_sem=rim_recv.at[k, 1 - side],
            device_id={"row": r + 2 * side - 1},
            device_id_type=MESH,
        )

    def rim_arrival(k, side):
        return pltpu.make_async_remote_copy(
            src_ref=rim_out.at[k, 1 - side],
            dst_ref=rim_in.at[k, side],
            send_sem=rim_send.at[k, 1 - side],
            recv_sem=rim_recv.at[k, side],
            device_id={"row": r + 2 * side - 1},
            device_id_type=MESH,
        )

    def psi_copy(side):
        return pltpu.make_async_remote_copy(
            src_ref=psi.at[:, ends[side]],
            dst_ref=psi_rim.at[1 - side],
            send_sem=psi_send.at[side],
            recv_sem=psi_recv.at[1 - side],
            device_id={"row": r + 2 * side - 1},
            device_id_type=MESH,
        )

    def psi_arrival(side):
        return pltpu.make_async_remote_copy(
            src_ref=psi.at[:, ends[1 - side]],
            dst_ref=psi_rim.at[side],
            send_sem=psi_send.at[1 - side],
            recv_sem=psi_recv.at[side],
            device_id={"row": r + 2 * side - 1},
            device_id_type=MESH,
        )

    def rim_sums(k, slot):
        for c in range(2):
            low, high = rim_rounded(slot, c, 0), rim_rounded(slot, c, 1)
            for side in range(2):
                part = partial[side, c * GROUPS : (c + 1) * GROUPS]
                rim_out[k, side, c] = part + corner[side][0] * low + corner[side][1] * high

    def send_rims(k):
        for side in range(2):

            @pl.when(has_row[side])
            def _():
                rim_copy(k, side).start()

    bufs = (below, above)

    def bulk_copy(side, i):
        return pltpu.make_async_remote_copy(
            src_ref=psi.at[:, pl.ds(i * CHUNK, CHUNK)],
            dst_ref=bufs[1 - side].at[:, pl.ds(i * CHUNK, CHUNK)],
            send_sem=bulk_send.at[side, i],
            recv_sem=bulk_recv.at[1 - side, i],
            device_id={"al": a + 2 * side - 1},
            device_id_type=MESH,
        )

    def bulk_arrival(side, i):
        return pltpu.make_async_remote_copy(
            src_ref=psi.at[:, pl.ds(i * CHUNK, CHUNK)],
            dst_ref=bufs[side].at[:, pl.ds(i * CHUNK, CHUNK)],
            send_sem=bulk_send.at[1 - side, i],
            recv_sem=bulk_recv.at[side, i],
            device_id={"al": a + 2 * side - 1},
            device_id_type=MESH,
        )

    def width_copy(j, source, target, peer):
        return pltpu.make_async_remote_copy(
            src_ref=source,
            dst_ref=target,
            send_sem=w_send.at[j],
            recv_sem=w_recv.at[j],
            device_id={"row": peer},
            device_id_type=MESH,
        )

    quad_copies = [width_copy(j, w_own, w_quad.at[j], quad_peers[j]) for j in range(QUAD - 1)]
    y_copies = [
        width_copy(QUAD - 1 + j, w_total, w_ys.at[j], y_peers[j]) for j in range(quads - 1)
    ]

    rim_sums(0, 0)
    fetch_acc.wait()
    degree = QUAD - 1 + quads - 1
    for present in has_al + has_row:
        degree = degree + present.astype(jnp.int32)
    pl.semaphore_wait(barrier, degree)

    for copy in quad_copies:
        copy.start()
    for side in range(2):

        @pl.when(has_row[side])
        def _():
            psi_copy(side).start()

    send_rims(0)
    for i in range(CHUNKS):
        for side in range(2):

            @pl.when(has_al[side])
            def _():
                bulk_copy(side, i).start()

    total = w_own[...]
    lower = jnp.zeros((8, 128), jnp.int32)
    for j, copy in enumerate(quad_copies):
        copy.wait_recv()
        got = w_quad[j]
        total = total + got
        lower = lower + jnp.where((q + QUAD - 1 - j) % QUAD < q, got, 0)
    w_total[...] = total
    for copy in y_copies:
        copy.start()
    for j, copy in enumerate(y_copies):
        copy.wait_recv()
        lower = lower + jnp.where((y + quads - 1 - j) % quads < y, w_ys[j], 0)
    edge = lower.astype(F32)
    tile = (P_SIZE // 8, R2 // 128)
    nodes = iota((P_SIZE, R2), 0).astype(F32) / (P_SIZE - 1)
    radius_one = radius_zero + jnp.tile(edge, tile) + jnp.tile(wide, tile) * nodes
    radius_two = radius_zero + radial_step * iota((P_SIZE, R2), 1).astype(F32)
    level_rows = jnp.full((P_SIZE, R2), a, jnp.int32).astype(F32)
    cent_one = level_rows * (level_rows + 1.0) / (2.0 * radius_one * radius_one) - 2.0 / radius_one
    potn[...] = cent_one + 1.0 / jnp.maximum(radius_one, radius_two)
    reach[...] = field[0] * radius_one / dipole_scale

    def fill_pot(n, _):
        pot[n] = cent2[...] + potn[pl.ds(n, 1)][None]
        return 0

    lax.fori_loop(0, P_SIZE, fill_pot, 0)

    def blocks_of(k, old, new):
        factor = dt_step / k

        def one(block, _):
            c, g = block // GROUPS, block % GROUPS
            xb = xbs[old, block]
            inner = dot(ke[...], xb)
            outer = dot(xb, outer_m[...])
            rest = outer + pot[:, g].reshape(ROWS, R2) * xs[old, c, :, g].reshape(ROWS, R2)
            op[0, block] = rest[0:SUB]
            op[1, block] = rest[ROWS - SUB :]
            image = (inner * scale + rest) * jnp.where(c == 1, factor, -factor)
            d = 1 - c
            image3 = image.reshape(P_SIZE, SUB, R2)
            xs[new, d, :, g] = image3
            inner_planes = slice(1, P_SIZE - 1)
            out[d, inner_planes, g] = out[d, inner_planes, g] + image3[inner_planes]
            if k < ORDER:
                target = d * GROUPS + g
                xbs[new, target] = image.astype(BF16)
                partial_sums(new, target)
            return 0

        lax.fori_loop(0, 2 * GROUPS, one, 0)

    def mix_chunk(i):
        rows = pl.ds(i * CHUNK, CHUNK)

        def one(c, _):
            mixed = jnp.zeros((MIXROWS, R2), F32)
            for side in range(2):
                value = bufs[side][c, rows].reshape(MIXROWS, R2)
                high = value.astype(BF16)
                low = (value - high.astype(F32)).astype(BF16)
                mixed = mixed + weights[side] * (dot(mix[side], high) + dot(mix[side], low))
            sign = jnp.where(c == 1, 1.0, -1.0)
            mixed = mixed.reshape(CHUNK, GROUPS, SUB, R2)
            far = reach[rows][:, None, None, :] * sign
            out[1 - c, rows] = out[1 - c, rows] + far * mixed
            return 0

        lax.fori_loop(0, 2, one, 0)

    def receive_chunk(i):
        for side in range(2):

            @pl.when(has_al[side])
            def _():
                bulk_arrival(side, i).wait_recv()

        mix_chunk(i)

    def finish_rims(k, old, new):
        factor = dt_step / k
        for side in range(2):

            @pl.when(has_row[side])
            def _():
                rim_arrival(k - 1, side).wait_recv()

        for c in range(2):
            for side in range(2):
                mine = op[side, c * GROUPS : (c + 1) * GROUPS]
                if k == 1:
                    theirs = psi_op[side][c]
                else:
                    theirs = mine
                raw = (rim_out[k - 1, side, c] + rim_in[k - 1, side, c]) + (mine + theirs)
                raw = jnp.where(has_row[side], raw, 0.0)
                xs[new, 1 - c, ends[side]] = raw * (factor if c == 1 else -factor)
        if k < ORDER:
            rim_sums(k, new)
            send_rims(k)
        for c in range(2):
            for end in ends:
                out[c, end] = out[c, end] + xs[new, c, end]
            if k < ORDER:
                for g in range(GROUPS):
                    for first, place in ((0, 0), (P_SIZE - 2, ROWS - 2 * SUB)):
                        pair = xs[new, c, first : first + 2, g].reshape(2 * SUB, R2)
                        xbs[new, c * GROUPS + g, place : place + 2 * SUB] = pair.astype(BF16)

    blocks_of(1, 0, 1)
    psi_op = []
    for side in range(2):

        @pl.when(has_row[side])
        def _():
            psi_arrival(side).wait_recv()

        parts = []
        for c in range(2):
            other = psi_rim[side, c]
            there = dot(other.reshape(L2, R2).astype(BF16), outer_m[...])
            parts.append(there.reshape(GROUPS, SUB, R2) + pot[ends[side]] * other)
        psi_op.append(parts)
    finish_rims(1, 0, 1)
    for k in range(2, ORDER + 1):
        old, new = (k - 1) % 2, k % 2
        blocks_of(k, old, new)
        if k == 3:
            receive_chunk(0)
        if k == 4:
            receive_chunk(1)
        finish_rims(k, old, new)
    for i in range(2, CHUNKS):
        receive_chunk(i)

    for copy in quad_copies + y_copies:
        copy.wait_send()
    for side in range(2):

        @pl.when(has_row[side])
        def _():
            psi_copy(side).wait_send()
            for k in range(ORDER):
                rim_copy(k, side).wait_send()

        @pl.when(has_al[side])
        def _():
            for i in range(CHUNKS):
                bulk_copy(side, i).wait_send()


def local(al_size, row_size, psi, angular, widths, field, elem_matrix, outer_matrix):
    shape = (2, P_SIZE, GROUPS, SUB, R2)
    plane = (GROUPS, SUB, R2)
    quads = row_size // QUAD
    dma = pltpu.SemaphoreType.DMA
    vmem = pl.BlockSpec(memory_space=pltpu.VMEM)
    smem = pl.BlockSpec(memory_space=pltpu.SMEM)
    hbm = pl.BlockSpec(memory_space=pl.ANY)
    blocks = 2 * GROUPS
    advanced = pl.pallas_call(
        functools.partial(kernel, al_size, row_size),
        out_shape=jax.ShapeDtypeStruct(shape, F32),
        in_specs=[hbm, vmem, smem, smem, vmem, hbm],
        out_specs=vmem,
        scratch_shapes=[
            pltpu.VMEM((2,) + shape, F32),
            pltpu.VMEM((2, blocks, ROWS, R2), BF16),
            pltpu.VMEM((P_SIZE,) + plane, F32),
            pltpu.VMEM(shape, F32),
            pltpu.VMEM(shape, F32),
            pltpu.VMEM((R2, R2), BF16),
            pltpu.VMEM((ROWS, ROWS), BF16),
            pltpu.VMEM((2 * SUB, ROWS), BF16),
            pltpu.VMEM((2, MIXROWS, MIXROWS), BF16),
            pltpu.VMEM(plane, F32),
            pltpu.VMEM((P_SIZE, R2), F32),
            pltpu.VMEM((P_SIZE, R2), F32),
            pltpu.VMEM((2, 2) + plane, F32),
            pltpu.VMEM((ORDER, 2, 2) + plane, F32),
            pltpu.VMEM((ORDER, 2, 2) + plane, F32),
            pltpu.VMEM((2, blocks, SUB, R2), F32),
            pltpu.VMEM((2, blocks, SUB, R2), F32),
            pltpu.VMEM((8, 128), jnp.int32),
            pltpu.VMEM((QUAD - 1, 8, 128), jnp.int32),
            pltpu.VMEM((8, 128), jnp.int32),
            pltpu.VMEM((quads - 1, 8, 128), jnp.int32),
            dma((3,)),
            dma((2, CHUNKS)),
            dma((2, CHUNKS)),
            dma((ORDER, 2)),
            dma((ORDER, 2)),
            dma((2,)),
            dma((2,)),
            dma((QUAD + quads - 2,)),
            dma((QUAD + quads - 2,)),
        ],
        compiler_params=pltpu.CompilerParams(
            collective_id=0, has_side_effects=True, vmem_limit_bytes=48 * 1024 * 1024
        ),
    )(psi.reshape(shape), angular, widths, field, elem_matrix, outer_matrix)
    return advanced.reshape(psi.shape)


def solution(mesh):
    placed = (P("al", None, "row", None, None), P(), P("row"), P(), P(), P())
    return jax.shard_map(
        functools.partial(local, mesh.shape["al"], mesh.shape["row"]),
        mesh=mesh,
        in_specs=placed,
        out_specs=P("al", None, "row", None, None),
        check_vma=False,
    )
```

time: 257 us -> 88.6 us (0.34)
  the two profiles are of different devices: /device:TPU:89 before, /device:TPU:15 now
where the time goes in v1:
time: 88.6 us; the launch traced here: 88.3 us
  Pallas kernels  81.6 us (92%)
  local copies, waits for them, and re-layouts  5.34 us (6%)
  between operations  1.32 us (1%)
    pallas_call x1, Pallas kernels, local(): pl.pallas_call(functools.partial(kernel, al_size, row_size), out_shape=ja...  81.6 us
    unnamed x9, local copies, waits for them, and re-layouts  5.34 us

profile of v1, /device:TPU:15, one launch (start us, length us, event | category | flops | bytes accessed | tf_op | source)
XLA Modules:
  0.0 88.3 jit_solution(9753442449937468477)
XLA Ops:
  1.3 0.0 copy-start
  1.3 1.6 %copy-done = f32[1,2,32,16,512]{4,3,2,1,0:T(8,128)S(1)} copy-done((f32[1,2,32,16,512]{4,3,2,1,0:T(8,128)S(1)}, f32[1,2,32,16,512]{4,3,2,1,0:T(8,128)}, u32[]{:S(2)}) %copy-start) | copy-done | bytes 2097176
  2.9 0.0 copy-start.1
  2.9 1.0 %copy-done.1 = bf16[512,512]{1,0:T(8,128)(2,1)S(1)} copy-done((bf16[512,512]{1,0:T(8,128)(2,1)S(1)}, bf16[512,512]{1,0:T(8,128)(2,1)}, u32[]{:S(2)}) %copy-start.1) | copy-done | bytes 524312
  3.9 0.0 copy-start.2
  3.9 0.7 copy-done.2
  4.6 0.0 copy-start.3
  4.6 0.7 copy-done.3
  5.3 81.6 %shard_map.64 = f32[2,32,2,8,512]{4,3,2,1,0:T(8,128)S(1)} custom-call(f32[2,32,2,8,512]{4,3,2,1,0:T(8,128)S(1)} %bitcast.3, s32[16,16]{1,0:T(8,128)S(1)} %copy-done.2, s32[1]{0:T(128)S(6)} %copy.8.widths, f32[1]{0:T(128)S(6)} %copy.9.field, bf16[32,32]{1,0:T(8,128)(2,1)S(1)} %copy-done.3, bf16[512,512]{1,0:T(8,128)(2,1)S(1)} %copy-done.1), custom_call_target="tpu_custom_call" | custom-call | tf_op jit(solution)/shard_map/pallas_call | solution.py:451
  86.9 1.3 %copy.10 = f32[1,2,32,16,512]{4,3,2,1,0:T(8,128)} copy(f32[1,2,32,16,512]{4,3,2,1,0:T(8,128)S(1)} %bitcast.2) | data formatting | bytes 4194304
Async XLA Ops:
  1.3 1.6 %copy-start = (f32[1,2,32,16,512]{4,3,2,1,0:T(8,128)S(1)}, f32[1,2,32,16,512]{4,3,2,1,0:T(8,128)}, u32[]{:S(2)}) copy-start(f32[1,2,32,16,512]{4,3,2,1,0:T(8,128)} %param.6) | copy-start | bytes 6291460
  2.9 1.0 %copy-start.1 = (bf16[512,512]{1,0:T(8,128)(2,1)S(1)}, bf16[512,512]{1,0:T(8,128)(2,1)}, u32[]{:S(2)}) copy-start(bf16[512,512]{1,0:T(8,128)(2,1)} %outer_hbm.1) | copy-start | bytes 1572868
  3.9 0.7 copy-start.2
  4.6 0.7 copy-start.3

commit v2 on v1

--- a/solution.py
+++ b/solution.py
@@ -19,9 +19,13 @@
 GROUPS = L2 // SUB
 ROWS = P_SIZE * SUB
 QUAD = 4
-CHUNKS = 4
+CHUNKS = 16
 CHUNK = P_SIZE // CHUNKS
-MIXROWS = CHUNK * L2
+DIRECT = CHUNKS // 2
+MIXPLANES = 8
+MIXROWS = MIXPLANES * L2
+X_SIZE = 4
+PACE = 2
 
 dt_step = 0.35
 radius_zero = 8.0
@@ -63,23 +67,45 @@
 
 def kernel(
     al_size, row_size,
-    psi, ang, widths, field, elem, outer_hbm,
+    psi, ang_hbm, widths, field, elem_hbm, outer_hbm,
     out,
     xs, xbs, pot, below, above, outer_m, ke, kp, mix, cent2, potn, reach,
-    psi_rim, rim_in, rim_out, op, partial, w_own, w_quad, w_total, w_ys,
+    psi_rim, rim_in, rim_out, op, partial, w_own, w_quad, w_total, w_ys, ang, elem, held,
     local_sem, bulk_send, bulk_recv, rim_send, rim_recv, psi_send, psi_recv, w_send, w_recv,
+    held_recv, pass_send,
 ):
     a = lax.axis_index("al")
     r = lax.axis_index("row")
     quads = row_size // QUAD
     q = r % QUAD
     y = r // QUAD
+    x = a % X_SIZE
     has_al = (a > 0, a < al_size - 1)
+    wraps = (has_al[0] & (x == 0), has_al[1] & (x == X_SIZE - 1))
+    at_end = (x == 0) | (x == X_SIZE - 1)
+    inward = jnp.where(x == 0, 1, -1)
+    passes = at_end & (a + inward * X_SIZE >= 0) & (a + inward * X_SIZE < al_size)
+    pass_from = a + inward * (X_SIZE - 1)
+    pass_to = a + inward * X_SIZE
+    pass_side = (passes & (x == X_SIZE - 1), passes & (x == 0))
+    al_peers = [
+        (has_al[0], a - 1),
+        (has_al[1], a + 1),
+        (at_end & (a >= X_SIZE), a - X_SIZE),
+        (at_end & (a < al_size - X_SIZE), a + X_SIZE),
+        (at_end, a + inward * (X_SIZE - 1)),
+    ]
     has_row = (r > 0, r < row_size - 1)
 
     fetch_psi = pltpu.make_async_copy(psi, xs.at[0], local_sem.at[0])
     fetch_acc = pltpu.make_async_copy(psi, out, local_sem.at[1])
     fetch_outer = pltpu.make_async_copy(outer_hbm, outer_m, local_sem.at[2])
+    fetch_small = [
+        pltpu.make_async_copy(elem_hbm, elem, local_sem.at[3]),
+        pltpu.make_async_copy(ang_hbm, ang, local_sem.at[4]),
+    ]
+    for fetch in fetch_small:
+        fetch.start()
     fetch_psi.start()
     fetch_outer.start()
     fetch_acc.start()
@@ -92,17 +118,21 @@
     for side in range(2):
         step = 2 * side - 1
 
-        @pl.when(has_al[side])
-        def _():
-            pl.semaphore_signal(barrier, inc=1, device_id={"al": a + step}, device_id_type=MESH)
-
         @pl.when(has_row[side])
         def _():
             pl.semaphore_signal(barrier, inc=1, device_id={"row": r + step}, device_id_type=MESH)
+
+    for present, peer in al_peers:
+
+        @pl.when(present)
+        def _():
+            pl.semaphore_signal(barrier, inc=1, device_id={"al": peer}, device_id_type=MESH)
 
     w_own[...] = jnp.full((8, 128), widths[0], jnp.int32)
     wide = jnp.full((8, 128), widths[0], jnp.int32).astype(F32)
     scale = jnp.max(4.0 / (wide * wide))
+    for fetch in fetch_small:
+        fetch.wait()
     ef = elem[...].astype(F32)
     ri, ci = iota((P_SIZE, P_SIZE), 0), iota((P_SIZE, P_SIZE), 1)
     ends = (0, P_SIZE - 1)
@@ -238,6 +268,68 @@
             device_id_type=MESH,
         )
 
+    def relay_copy(side, i):
+        ahead = (2 * side - 1) * (1 - X_SIZE)
+        return pltpu.make_async_remote_copy(
+            src_ref=psi.at[:, pl.ds(i * CHUNK, CHUNK)],
+            dst_ref=held.at[i - DIRECT],
+            send_sem=bulk_send.at[side, i],
+            recv_sem=held_recv.at[i - DIRECT],
+            device_id={"al": a + ahead},
+            device_id_type=MESH,
+        )
+
+    def pass_copy(side, i):
+        return pltpu.make_async_remote_copy(
+            src_ref=held.at[i - DIRECT],
+            dst_ref=bufs[1 - side].at[:, pl.ds(i * CHUNK, CHUNK)],
+            send_sem=pass_send.at[i - DIRECT],
+            recv_sem=bulk_recv.at[1 - side, i],
+            device_id={"al": pass_to},
+            device_id_type=MESH,
+        )
+
+    def pass_on(turn):
+        for i in range(DIRECT + PACE * turn, DIRECT + PACE * (turn + 1)):
+
+            @pl.when(passes)
+            def _():
+                pltpu.make_async_remote_copy(
+                    src_ref=psi.at[:, pl.ds(i * CHUNK, CHUNK)],
+                    dst_ref=held.at[i - DIRECT],
+                    send_sem=bulk_send.at[0, i],
+                    recv_sem=held_recv.at[i - DIRECT],
+                    device_id={"al": pass_from},
+                    device_id_type=MESH,
+                ).wait_recv()
+
+            for side in range(2):
+
+                @pl.when(pass_side[side])
+                def _():
+                    pass_copy(side, i).start()
+
+    def start_bulk():
+        for side in range(2):
+
+            @pl.when(has_al[side] & jnp.logical_not(wraps[side]))
+            def _():
+                for i in range(CHUNKS):
+                    bulk_copy(side, i).start()
+
+            @pl.when(wraps[side])
+            def _():
+                for i in range(DIRECT, CHUNKS):
+                    relay_copy(side, i).start()
+
+    def start_direct(turn):
+        for side in range(2):
+
+            @pl.when(wraps[side])
+            def _():
+                for i in range(PACE * turn, PACE * (turn + 1)):
+                    bulk_copy(side, i).start()
+
     def bulk_arrival(side, i):
         return pltpu.make_async_remote_copy(
             src_ref=psi.at[:, pl.ds(i * CHUNK, CHUNK)],
@@ -266,7 +358,7 @@
     rim_sums(0, 0)
     fetch_acc.wait()
     degree = QUAD - 1 + quads - 1
-    for present in has_al + has_row:
+    for present in [present for present, _ in al_peers] + list(has_row):
         degree = degree + present.astype(jnp.int32)
     pl.semaphore_wait(barrier, degree)
 
@@ -279,12 +371,8 @@
             psi_copy(side).start()
 
     send_rims(0)
-    for i in range(CHUNKS):
-        for side in range(2):
-
-            @pl.when(has_al[side])
-            def _():
-                bulk_copy(side, i).start()
+    start_bulk()
+    start_direct(0)
 
     total = w_own[...]
     lower = jnp.zeros((8, 128), jnp.int32)
@@ -340,32 +428,35 @@
 
         lax.fori_loop(0, 2 * GROUPS, one, 0)
 
-    def mix_chunk(i):
-        rows = pl.ds(i * CHUNK, CHUNK)
+    def mix_planes(first, count):
+        rows = pl.ds(first, count)
+        size = count * L2
 
         def one(c, _):
-            mixed = jnp.zeros((MIXROWS, R2), F32)
+            mixed = jnp.zeros((size, R2), F32)
             for side in range(2):
-                value = bufs[side][c, rows].reshape(MIXROWS, R2)
+                value = bufs[side][c, rows].reshape(size, R2)
                 high = value.astype(BF16)
                 low = (value - high.astype(F32)).astype(BF16)
-                mixed = mixed + weights[side] * (dot(mix[side], high) + dot(mix[side], low))
+                match = mix[side, 0:size, 0:size]
+                mixed = mixed + weights[side] * (dot(match, high) + dot(match, low))
             sign = jnp.where(c == 1, 1.0, -1.0)
-            mixed = mixed.reshape(CHUNK, GROUPS, SUB, R2)
+            mixed = mixed.reshape(count, GROUPS, SUB, R2)
             far = reach[rows][:, None, None, :] * sign
             out[1 - c, rows] = out[1 - c, rows] + far * mixed
             return 0
 
         lax.fori_loop(0, 2, one, 0)
 
-    def receive_chunk(i):
-        for side in range(2):
-
-            @pl.when(has_al[side])
-            def _():
-                bulk_arrival(side, i).wait_recv()
-
-        mix_chunk(i)
+    def receive_planes(first, count):
+        for i in range(first // CHUNK, (first + count) // CHUNK):
+            for side in range(2):
+
+                @pl.when(has_al[side])
+                def _():
+                    bulk_arrival(side, i).wait_recv()
+
+        mix_planes(first, count)
 
     def finish_rims(k, old, new):
         factor = dt_step / k
@@ -413,15 +504,18 @@
         psi_op.append(parts)
     finish_rims(1, 0, 1)
     for k in range(2, ORDER + 1):
+        start_direct(k - 1)
+        pass_on(k - 2)
         old, new = (k - 1) % 2, k % 2
         blocks_of(k, old, new)
-        if k == 3:
-            receive_chunk(0)
         if k == 4:
-            receive_chunk(1)
+            receive_planes(0, 8)
         finish_rims(k, old, new)
-    for i in range(2, CHUNKS):
-        receive_chunk(i)
+    pass_on(ORDER - 1)
+    receive_planes(8, 8)
+    receive_planes(16, 8)
+    receive_planes(24, 4)
+    receive_planes(28, 4)
 
     for copy in quad_copies + y_copies:
         copy.wait_send()
@@ -437,6 +531,11 @@
         def _():
             for i in range(CHUNKS):
                 bulk_copy(side, i).wait_send()
+
+        @pl.when(pass_side[side])
+        def _():
+            for i in range(DIRECT, CHUNKS):
+                pass_copy(side, i).wait_send()
 
 
 def local(al_size, row_size, psi, angular, widths, field, elem_matrix, outer_matrix):
@@ -446,12 +545,12 @@
     dma = pltpu.SemaphoreType.DMA
     vmem = pl.BlockSpec(memory_space=pltpu.VMEM)
     smem = pl.BlockSpec(memory_space=pltpu.SMEM)
-    hbm = pl.BlockSpec(memory_space=pl.ANY)
+    hbm = pl.BlockSpec(memory_space=pltpu.HBM)
     blocks = 2 * GROUPS
     advanced = pl.pallas_call(
         functools.partial(kernel, al_size, row_size),
         out_shape=jax.ShapeDtypeStruct(shape, F32),
-        in_specs=[hbm, vmem, smem, smem, vmem, hbm],
+        in_specs=[hbm, hbm, smem, smem, hbm, hbm],
         out_specs=vmem,
         scratch_shapes=[
             pltpu.VMEM((2,) + shape, F32),
@@ -475,7 +574,10 @@
             pltpu.VMEM((QUAD - 1, 8, 128), jnp.int32),
             pltpu.VMEM((8, 128), jnp.int32),
             pltpu.VMEM((quads - 1, 8, 128), jnp.int32),
-            dma((3,)),
+            pltpu.VMEM((L2, L2), jnp.int32),
+            pltpu.VMEM((P_SIZE, P_SIZE), BF16),
+            pltpu.VMEM((CHUNKS - DIRECT, 2, CHUNK) + plane, F32),
+            dma((5,)),
             dma((2, CHUNKS)),
             dma((2, CHUNKS)),
             dma((ORDER, 2)),
@@ -484,11 +586,13 @@
             dma((2,)),
             dma((QUAD + quads - 2,)),
             dma((QUAD + quads - 2,)),
+            dma((CHUNKS - DIRECT,)),
+            dma((CHUNKS - DIRECT,)),
         ],
         compiler_params=pltpu.CompilerParams(
             collective_id=0, has_side_effects=True, vmem_limit_bytes=48 * 1024 * 1024
         ),
-    )(psi.reshape(shape), angular, widths, field, elem_matrix, outer_matrix)
+    )(*[pltpu.with_memory_space_constraint(v, pltpu.HBM) if i in (0,1,4,5) else v for i,v in enumerate((psi.reshape(shape), angular, widths, field, elem_matrix, outer_matrix))])
     return advanced.reshape(psi.shape)
 
 

time: 88.6 us -> 66.1 us (0.75)
  the two profiles are of different devices: /device:TPU:15 before, /device:TPU:62 now
where the time goes in v2:
time: 66.1 us; the launch traced here: 65.9 us
  Pallas kernels  63.3 us (96%)
  local copies, waits for them, and re-layouts  1.32 us (2%)
  between operations  1.3 us (2%)
    pallas_call x1, Pallas kernels, local(): pl.pallas_call(functools.partial(kernel, al_size, row_size), out_shape=ja...  63.3 us

profile of v2, /device:TPU:62, one launch (start us, length us, event | category | flops | bytes accessed | tf_op | source)
XLA Modules:
  0.0 65.9 jit_solution(10850852490224556403)
XLA Ops:
  1.3 63.3 %shard_map.64 = f32[2,32,2,8,512]{4,3,2,1,0:T(8,128)S(1)} custom-call(f32[2,32,2,8,512]{4,3,2,1,0:T(8,128)} %bitcast.3, s32[16,16]{1,0:T(8,128)} %ang_hbm.1, s32[1]{0:T(128)S(6)} %copy.8.widths, f32[1]{0:T(128)S(6)} %copy.9.field, bf16[32,32]{1,0:T(8,128)(2,1)} %elem_hbm.1, bf16[512,512]{1,0:T(8,128)(2,1)} %outer_hbm.1), custom_call_target="tpu_custom_call" | custom-call | tf_op jit(solution)/shard_map/pallas_call | solution.py:550
  64.6 1.3 %copy.10 = f32[1,2,32,16,512]{4,3,2,1,0:T(8,128)} copy(f32[1,2,32,16,512]{4,3,2,1,0:T(8,128)S(1)} %bitcast.2) | data formatting | bytes 4194304

commit v3 on v1

v3 whole, which is shorter than its diff:
```python
import functools

import jax
import jax.numpy as jnp
from jax import lax
from jax.experimental import pallas as pl
from jax.experimental.pallas import tpu as pltpu
from jax.sharding import PartitionSpec as P

MESH = pl.DeviceIdType.MESH
F32 = jnp.float32
BF16 = jnp.bfloat16

P_SIZE = 32
L2 = 16
R2 = 512
ORDER = 4
SUB = 8
GROUPS = L2 // SUB
ROWS = P_SIZE * SUB
QUAD = 4
CHUNKS = P_SIZE
CHUNK = P_SIZE // CHUNKS
DIRECT = CHUNKS // 2
MIXPLANES = 8
MIXROWS = MIXPLANES * L2
X_SIZE = 4
CHAINS = 2 * GROUPS
BIG = 4

dt_step = 0.35
radius_zero = 8.0
radial_step = 0.25
dipole_scale = 64.0


def iota(shape, dim):
    return lax.broadcasted_iota(jnp.int32, shape, dim)


def dot(a, b):
    return jnp.dot(a, b, preferred_element_type=F32)


def dot_lhs_t(a, b):
    return lax.dot_general(a, b, (((0,), (0,)), ((), ())), preferred_element_type=F32)


def ones_where(mask):
    return jnp.where(mask, 1.0, 0.0).astype(BF16)


def spread(size, inner, count):
    rows = iota((size, count), 0)
    rows = rows // inner if inner else rows % count
    return ones_where(rows == iota((size, count), 1))


def spread_t(size, inner, count):
    cols = iota((count, size), 1)
    cols = cols // inner if inner else cols % count
    return ones_where(cols == iota((count, size), 0))


def coupling_weight(level):
    return (level + 1.0) / jnp.sqrt((2.0 * level + 1.0) * (2.0 * level + 3.0))


def kernel(
    al_size, row_size,
    psi, ang_hbm, widths, field, elem_hbm, outer_hbm,
    out,
    xs, xbs, pot, below, above, outer_m, ke, kp, mix, cent2, potn, reach,
    psi_rim, rim_in, rim_out, op, op_there, partial, w_own, w_quad, w_total, w_ys, ang, elem, held, held_z,
    local_sem, bulk_send, bulk_recv, rim_send, rim_recv, psi_send, psi_recv, w_send, w_recv,
    held_recv, pass_send, held_z_recv, pass_z_send,
    near_sem, twice_sem, row_sem,
):
    a = lax.axis_index("al")
    r = lax.axis_index("row")
    quads = row_size // QUAD
    q = r % QUAD
    y = r // QUAD
    x = a % X_SIZE
    has_al = (a > 0, a < al_size - 1)
    wraps = (has_al[0] & (x == 0), has_al[1] & (x == X_SIZE - 1))
    at_end = (x == 0) | (x == X_SIZE - 1)
    inward = jnp.where(x == 0, 1, -1)
    passes = at_end & (a + inward * X_SIZE >= 0) & (a + inward * X_SIZE < al_size)
    pass_from = a + inward * (X_SIZE - 1)
    pass_to = a + inward * X_SIZE
    pass_side = (passes & (x == X_SIZE - 1), passes & (x == 0))
    pass_z_side = (pass_side[1], pass_side[0])
    has_row = (r > 0, r < row_size - 1)
    odd = x % 2 == 1
    even = jnp.logical_not(odd)
    al_peers = [(has_al[0], a - 1), (has_al[1], a + 1), (at_end, a + inward * (X_SIZE - 1))]

    fetch_psi = pltpu.make_async_copy(psi, xs.at[0], local_sem.at[0])
    fetch_acc = pltpu.make_async_copy(psi, out, local_sem.at[1])
    fetch_outer = pltpu.make_async_copy(outer_hbm, outer_m, local_sem.at[2])
    fetch_small = [
        pltpu.make_async_copy(elem_hbm, elem, local_sem.at[3]),
        pltpu.make_async_copy(ang_hbm, ang, local_sem.at[4]),
    ]
    for fetch in fetch_small:
        fetch.start()
    fetch_psi.start()
    fetch_outer.start()
    fetch_acc.start()

    barrier = pltpu.get_barrier_semaphore()
    quad_peers = [y * QUAD + (q + j) % QUAD for j in range(1, QUAD)]
    y_peers = [((y + j) % quads) * QUAD + q for j in range(1, quads)]

    def signal_al(sem):
        for present, peer in al_peers:

            @pl.when(present)
            def _():
                pl.semaphore_signal(sem, inc=1, device_id={"al": peer}, device_id_type=MESH)

    al_count = 0
    for present, _ in al_peers:
        al_count = al_count + present.astype(jnp.int32)
    row_count = QUAD - 1 + quads - 1
    for present in has_row:
        row_count = row_count + present.astype(jnp.int32)

    @pl.when(odd)
    def _():
        signal_al(barrier)

    w_own[...] = jnp.full((8, 128), widths[0], jnp.int32)
    ends = (0, P_SIZE - 1)

    def partial_sums(xb, chain):
        sums = dot(kp[...], xb) * scale
        partial[0, chain] = sums[0:SUB]
        partial[1, chain] = sums[SUB:]

    def round_start(chain, _):
        c, g = chain // GROUPS, chain % GROUPS
        xb = xs[0, c, :, g].reshape(ROWS, R2).astype(BF16)
        xbs[0, chain] = xb
        partial_sums(xb, chain)
        rim_sums(0, chain, [xs[0, c, end, g] for end in ends])
        return 0

    def rim_copy(k, side, chain):
        return pltpu.make_async_remote_copy(
            src_ref=rim_out.at[k, side, chain],
            dst_ref=rim_in.at[k, 1 - side, chain],
            send_sem=rim_send.at[k, side, chain],
            recv_sem=rim_recv.at[k, 1 - side, chain],
            device_id={"row": r + 2 * side - 1},
            device_id_type=MESH,
        )

    def rim_arrival(k, side, chain):
        return pltpu.make_async_remote_copy(
            src_ref=rim_out.at[k, 1 - side, chain],
            dst_ref=rim_in.at[k, side, chain],
            send_sem=rim_send.at[k, 1 - side, chain],
            recv_sem=rim_recv.at[k, side, chain],
            device_id={"row": r + 2 * side - 1},
            device_id_type=MESH,
        )

    def psi_copy(side):
        return pltpu.make_async_remote_copy(
            src_ref=psi.at[:, ends[side]],
            dst_ref=psi_rim.at[1 - side],
            send_sem=psi_send.at[side],
            recv_sem=psi_recv.at[1 - side],
            device_id={"row": r + 2 * side - 1},
            device_id_type=MESH,
        )

    def psi_arrival(side):
        return pltpu.make_async_remote_copy(
            src_ref=psi.at[:, ends[1 - side]],
            dst_ref=psi_rim.at[side],
            send_sem=psi_send.at[1 - side],
            recv_sem=psi_recv.at[side],
            device_id={"row": r + 2 * side - 1},
            device_id_type=MESH,
        )

    def rim_sums(k, chain, rims):
        rounded = [rim.astype(BF16).astype(F32) for rim in rims]
        for side in range(2):
            lows, highs = [corner[side][end] * rounded[end] for end in range(2)]
            rim_out[k, side, chain] = partial[side, chain] + lows + highs

    def send_rims(k, chain):
        for side in range(2):

            @pl.when(has_row[side])
            def _():
                rim_copy(k, side, chain).start()

    bufs = (below, above)

    def bulk_copy(side, j):
        return pltpu.make_async_remote_copy(
            src_ref=psi.at[:, pl.ds(j * BIG, BIG)],
            dst_ref=bufs[1 - side].at[:, pl.ds(j * BIG, BIG)],
            send_sem=bulk_send.at[side, j],
            recv_sem=bulk_recv.at[1 - side, j],
            device_id={"al": a + 2 * side - 1},
            device_id_type=MESH,
        )

    def relay_copy(side, i):
        ahead = (2 * side - 1) * (1 - X_SIZE)
        return pltpu.make_async_remote_copy(
            src_ref=psi.at[:, pl.ds(i * CHUNK, CHUNK)],
            dst_ref=held.at[i - DIRECT],
            send_sem=bulk_send.at[side, i],
            recv_sem=held_recv.at[i - DIRECT],
            device_id={"al": a + ahead},
            device_id_type=MESH,
        )

    def pass_copy(side, i):
        return pltpu.make_async_remote_copy(
            src_ref=held.at[i - DIRECT],
            dst_ref=bufs[1 - side].at[:, pl.ds(i * CHUNK, CHUNK)],
            send_sem=pass_send.at[i - DIRECT],
            recv_sem=bulk_recv.at[1 - side, i],
            device_id={"al": pass_to},
            device_id_type=MESH,
        )

    def pass_on(i):
        @pl.when(passes)
        def _():
            pltpu.make_async_remote_copy(
                src_ref=psi.at[:, pl.ds(i * CHUNK, CHUNK)],
                dst_ref=held.at[i - DIRECT],
                send_sem=bulk_send.at[0, i],
                recv_sem=held_recv.at[i - DIRECT],
                device_id={"al": pass_from},
                device_id_type=MESH,
            ).wait_recv()

        for side in range(2):

            @pl.when(pass_side[side])
            def _():
                pass_copy(side, i).start()

    def ahead_copy(side, i):
        return pltpu.make_async_remote_copy(
            src_ref=psi.at[:, pl.ds(i * CHUNK, CHUNK)],
            dst_ref=held_z.at[i],
            send_sem=bulk_send.at[side, i],
            recv_sem=held_z_recv.at[i],
            device_id={"al": a + (2 * side - 1) * X_SIZE},
            device_id_type=MESH,
        )

    def pass_z_copy(side, i):
        return pltpu.make_async_remote_copy(
            src_ref=held_z.at[i],
            dst_ref=bufs[1 - side].at[:, pl.ds(i * CHUNK, CHUNK)],
            send_sem=pass_z_send.at[i],
            recv_sem=bulk_recv.at[1 - side, i],
            device_id={"al": pass_from},
            device_id_type=MESH,
        )

    def pass_z_on(i):
        @pl.when(passes)
        def _():
            pltpu.make_async_remote_copy(
                src_ref=psi.at[:, pl.ds(i * CHUNK, CHUNK)],
                dst_ref=held_z.at[i],
                send_sem=bulk_send.at[0, i],
                recv_sem=held_z_recv.at[i],
                device_id={"al": pass_to},
                device_id_type=MESH,
            ).wait_recv()

        for side in range(2):

            @pl.when(pass_z_side[side])
            def _():
                pass_z_copy(side, i).start()

    def over(first, last, act):
        def one(i, _):
            act(i)
            return 0

        lax.fori_loop(first, last, one, 0)

    def relay_part(side):
        def act(i):
            @pl.when(i >= DIRECT)
            def _():
                relay_copy(side, i).start()

        return act

    def start_pieces(j):
        for side in range(2):

            @pl.when(has_al[side] & jnp.logical_not(wraps[side]))
            def _():
                bulk_copy(side, j).start()

            @pl.when(wraps[side])
            def _():
                over(j * BIG, (j + 1) * BIG, relay_part(side))

    def start_ahead(i):
        for side in range(2):

            @pl.when(wraps[side])
            def _():
                ahead_copy(side, i).start()

    def arrival(side, first, count, sem):
        return pltpu.make_async_remote_copy(
            src_ref=psi.at[:, pl.ds(first, count)],
            dst_ref=bufs[side].at[:, pl.ds(first, count)],
            send_sem=bulk_send.at[1 - side, sem],
            recv_sem=bulk_recv.at[side, sem],
            device_id={"al": a + 2 * side - 1},
            device_id_type=MESH,
        )

    def width_copy(j, source, target, peer):
        return pltpu.make_async_remote_copy(
            src_ref=source,
            dst_ref=target,
            send_sem=w_send.at[j],
            recv_sem=w_recv.at[j],
            device_id={"row": peer},
            device_id_type=MESH,
        )

    quad_copies = [width_copy(j, w_own, w_quad.at[j], quad_peers[j]) for j in range(QUAD - 1)]
    y_copies = [
        width_copy(QUAD - 1 + j, w_total, w_ys.at[j], y_peers[j]) for j in range(quads - 1)
    ]

    @pl.when(even)
    def _():
        pl.semaphore_wait(barrier, al_count)
        signal_al(near_sem)

    @pl.when(odd)
    def _():
        pl.semaphore_wait(near_sem, al_count)
        signal_al(twice_sem)
        for peer in quad_peers + y_peers:
            pl.semaphore_signal(barrier, inc=1, device_id={"row": peer}, device_id_type=MESH)
        for side in range(2):

            @pl.when(has_row[side])
            def _():
                pl.semaphore_signal(
                    barrier, inc=1, device_id={"row": r + 2 * side - 1}, device_id_type=MESH
                )

    over(DIRECT // BIG, CHUNKS // BIG, start_pieces)
    over(0, DIRECT // BIG, start_pieces)

    @pl.when(even)
    def _():
        pl.semaphore_wait(twice_sem, al_count)

    over(0, 4, start_ahead)

    wide = jnp.full((8, 128), widths[0], jnp.int32).astype(F32)
    scale = jnp.max(4.0 / (wide * wide))
    for fetch in fetch_small:
        fetch.wait()
    ef = elem[...].astype(F32)
    ri, ci = iota((P_SIZE, P_SIZE), 0), iota((P_SIZE, P_SIZE), 1)
    corner = [[jnp.sum(jnp.where((ri == i) & (ci == k), ef, 0.0)) * scale for k in ends] for i in ends]
    wide_rows = dot(spread(ROWS, SUB, P_SIZE), elem[...]).astype(BF16)
    kron = dot(wide_rows, spread_t(ROWS, SUB, P_SIZE))
    kr, kc = iota((ROWS, ROWS), 0), iota((ROWS, ROWS), 1)
    kron = jnp.where(kr % SUB == kc % SUB, kron, 0.0)
    ke[...] = kron.astype(BF16)
    inside = (kc >= SUB) & (kc < ROWS - SUB)
    kron = jnp.where(inside, kron, 0.0)
    kp[...] = jnp.concatenate([kron[0:SUB], kron[ROWS - SUB :]], 0).astype(BF16)

    fetch_psi.wait()
    fetch_outer.wait()

    over(0, CHAINS, lambda chain: round_start(chain, 0))

    @pl.when(odd)
    def _():
        pl.semaphore_wait(barrier, row_count)
        pl.semaphore_signal(row_sem, inc=1, device_id={"al": a - 1}, device_id_type=MESH)

    @pl.when(even)
    def _():
        pl.semaphore_wait(row_sem, 1)

    for copy in quad_copies:
        copy.start()
    for side in range(2):

        @pl.when(has_row[side])
        def _():
            psi_copy(side).start()

    over(0, CHAINS, lambda chain: send_rims(0, chain))
    over(4, 7, start_ahead)
    over(DIRECT, DIRECT + 3, pass_on)

    angf = ang[...]
    slots = iota((L2, L2), 0)

    def one_hot(level):
        row = jnp.sum(jnp.where(slots == level, angf, 0), axis=0, keepdims=True)
        return ones_where(jnp.broadcast_to(row, (L2, L2)) == slots)

    own_hot = one_hot(a)
    mr, mc = iota((MIXROWS, MIXROWS), 0), iota((MIXROWS, MIXROWS), 1)
    for side in range(2):
        level = jnp.clip(a + 2 * side - 1, 0, al_size - 1)
        match = dot_lhs_t(own_hot, one_hot(level)).astype(BF16)
        tall = dot(spread(MIXROWS, 0, L2), match).astype(BF16)
        full = dot(tall, spread_t(MIXROWS, 0, L2))
        mix[side] = jnp.where(mr // L2 == mc // L2, full, 0.0).astype(BF16)
    momenta = iota((L2, R2), 0)
    square = dot_lhs_t(own_hot, (momenta * (momenta + 1)).astype(F32).astype(BF16))
    radius_two = radius_zero + radial_step * iota((L2, R2), 1).astype(F32)
    cent = square / (2.0 * radius_two * radius_two) - 2.0 / radius_two
    cent2[...] = cent.reshape(GROUPS, SUB, R2)

    level_one = jnp.full((8, 128), a, jnp.int32).astype(F32)
    weights = (
        jnp.max(coupling_weight(jnp.maximum(level_one - 1.0, 0.0))),
        jnp.max(coupling_weight(level_one)),
    )
    for side, buf in enumerate((below, above)):

        @pl.when(jnp.logical_not(has_al[side]))
        def _():
            def clear(n, _):
                for part in range(2):
                    buf[part, n] = jnp.zeros((GROUPS, SUB, R2), F32)
                return 0

            lax.fori_loop(0, P_SIZE, clear, 0)

    fetch_acc.wait()

    total = w_own[...]
    lower = jnp.zeros((8, 128), jnp.int32)
    for j, copy in enumerate(quad_copies):
        copy.wait_recv()
        got = w_quad[j]
        total = total + got
        lower = lower + jnp.where((q + QUAD - 1 - j) % QUAD < q, got, 0)
    w_total[...] = total
    for copy in y_copies:
        copy.start()
    for j, copy in enumerate(y_copies):
        copy.wait_recv()
        lower = lower + jnp.where((y + quads - 1 - j) % quads < y, w_ys[j], 0)
    over(0, 4, pass_z_on)
    edge = lower.astype(F32)
    tile = (P_SIZE // 8, R2 // 128)
    nodes = iota((P_SIZE, R2), 0).astype(F32) / (P_SIZE - 1)
    radius_one = radius_zero + jnp.tile(edge, tile) + jnp.tile(wide, tile) * nodes
    radius_two = radius_zero + radial_step * iota((P_SIZE, R2), 1).astype(F32)
    level_rows = jnp.full((P_SIZE, R2), a, jnp.int32).astype(F32)
    cent_one = level_rows * (level_rows + 1.0) / (2.0 * radius_one * radius_one) - 2.0 / radius_one
    potn[...] = cent_one + 1.0 / jnp.maximum(radius_one, radius_two)
    reach[...] = field[0] * radius_one / dipole_scale

    def fill_pot(n, _):
        pot[n] = cent2[...] + potn[pl.ds(n, 1)][None]
        return 0

    lax.fori_loop(0, P_SIZE, fill_pot, 0)

    def place(k, chain):
        return (chain // GROUPS + k) % 2, chain % GROUPS

    def inside_of(k, chain):
        old, new = (k - 1) % 2, k % 2
        factor = dt_step / k
        c, g = place(k - 1, chain)
        d = 1 - c
        xb = xbs[old, c * GROUPS + g]
        inner = dot(ke[...], xb)
        outer = dot(xb, outer_m[...])
        rest = outer + pot[:, g].reshape(ROWS, R2) * xs[old, c, :, g].reshape(ROWS, R2)
        op[0, chain] = rest[0:SUB]
        op[1, chain] = rest[ROWS - SUB :]
        image = (inner * scale + rest) * jnp.where(c == 1, factor, -factor)
        image3 = image.reshape(P_SIZE, SUB, R2)
        xs[new, d, :, g] = image3
        inner_planes = slice(1, P_SIZE - 1)
        out[d, inner_planes, g] = out[d, inner_planes, g] + image3[inner_planes]
        if k < ORDER:
            xb = image.astype(BF16)
            xbs[new, d * GROUPS + g] = xb
            partial_sums(xb, chain)

    def rims_of(k, chain):
        new = k % 2
        factor = dt_step / k
        c, g = place(k - 1, chain)
        d = 1 - c
        for side in range(2):

            @pl.when(has_row[side])
            def _():
                rim_arrival(k - 1, side, chain).wait_recv()

        rims = []
        for side in range(2):
            mine = op[side, chain]
            theirs = op_there[side, chain] if k == 1 else mine
            raw = (rim_out[k - 1, side, chain] + rim_in[k - 1, side, chain]) + (mine + theirs)
            raw = jnp.where(has_row[side], raw, 0.0)
            rims.append(raw * jnp.where(c == 1, factor, -factor))
        if k < ORDER:
            rim_sums(k, chain, rims)
            send_rims(k, chain)
        for rim, end in zip(rims, ends):
            xs[new, d, end, g] = rim
            out[d, end, g] = out[d, end, g] + rim
        if k < ORDER:
            for first, row in ((0, 0), (P_SIZE - 2, ROWS - 2 * SUB)):
                pair = xs[new, d, first : first + 2, g].reshape(2 * SUB, R2)
                xbs[new, d * GROUPS + g, row : row + 2 * SUB] = pair.astype(BF16)

    def mix_planes(first, count):
        rows = pl.ds(first, count)
        size = count * L2

        def one(c, _):
            mixed = jnp.zeros((size, R2), F32)
            for side in range(2):
                value = bufs[side][c, rows].reshape(size, R2)
                high = value.astype(BF16)
                low = (value - high.astype(F32)).astype(BF16)
                match = mix[side, 0:size, 0:size]
                mixed = mixed + weights[side] * (dot(match, high) + dot(match, low))
            sign = jnp.where(c == 1, 1.0, -1.0)
            mixed = mixed.reshape(count, GROUPS, SUB, R2)
            far = reach[rows][:, None, None, :] * sign
            out[1 - c, rows] = out[1 - c, rows] + far * mixed
            return 0

        lax.fori_loop(0, 2, one, 0)

    def receive_planes(first, count):
        for side in range(2):

            @pl.when(has_al[side] & jnp.logical_not(wraps[side]))
            def _():
                for j in range(first // BIG, (first + count) // BIG):
                    arrival(side, j * BIG, BIG, j).wait_recv()

            @pl.when(wraps[side])
            def _():
                over(first, first + count, lambda i: arrival(side, i, 1, i).wait_recv())

        mix_planes(first, count)

    for side in range(2):

        @pl.when(has_row[side])
        def _():
            psi_arrival(side).wait_recv()

    beyond = psi_rim[...]
    there = dot(beyond.reshape(2 * 2 * L2, R2).astype(BF16), outer_m[...])
    there = there.reshape(2, 2, GROUPS, SUB, R2)
    for side in range(2):
        added = there[side] + pot[ends[side]][None] * beyond[side]
        op_there[side] = added.reshape(CHAINS, SUB, R2)

    over(0, CHAINS, lambda chain: inside_of(1, chain))
    plan = (
        (start_ahead, (7, 9, 10, DIRECT)),
        (pass_on, (DIRECT + 3, DIRECT + 5, DIRECT + 7, CHUNKS)),
        (pass_z_on, (4, 6, 8, 10)),
    )
    for k in range(1, ORDER + 1):

        def step(chain):
            turn = CHAINS * (k - 1) + chain
            rims_of(k, chain)

            if k < ORDER:

                @pl.when(chain == CHAINS - 1)
                def _():
                    for act, bounds in plan:
                        over(bounds[k - 1], bounds[k], act)

            if k < ORDER:
                inside_of(k + 1, chain)

        over(0, CHAINS, step)
    over(10, 14, pass_z_on)
    receive_planes(16, 8)
    over(14, DIRECT, pass_z_on)
    for first, count in ((24, 8), (0, 8), (8, 4), (12, 4)):
        receive_planes(first, count)

    for copy in quad_copies + y_copies:
        copy.wait_send()
    for side in range(2):

        @pl.when(has_row[side])
        def _():
            psi_copy(side).wait_send()
            for k in range(ORDER):
                over(0, CHAINS, lambda chain: rim_copy(k, side, chain).wait_send())

        @pl.when(has_al[side] & jnp.logical_not(wraps[side]))
        def _():
            over(0, CHUNKS // BIG, lambda j: bulk_copy(side, j).wait_send())

        @pl.when(wraps[side])
        def _():
            over(DIRECT, CHUNKS, lambda i: relay_copy(side, i).wait_send())
            over(0, DIRECT, lambda i: ahead_copy(side, i).wait_send())

        @pl.when(pass_side[side])
        def _():
            over(DIRECT, CHUNKS, lambda i: pass_copy(side, i).wait_send())

        @pl.when(pass_z_side[side])
        def _():
            over(0, DIRECT, lambda i: pass_z_copy(side, i).wait_send())


def local(al_size, row_size, psi, angular, widths, field, elem_matrix, outer_matrix):
    shape = (2, P_SIZE, GROUPS, SUB, R2)
    plane = (GROUPS, SUB, R2)
    in_hbm = functools.partial(pltpu.with_memory_space_constraint, memory_space=pltpu.HBM)
    quads = row_size // QUAD
    dma = pltpu.SemaphoreType.DMA
    vmem = pl.BlockSpec(memory_space=pltpu.VMEM)
    smem = pl.BlockSpec(memory_space=pltpu.SMEM)
    hbm = pl.BlockSpec(memory_space=pltpu.HBM)
    advanced = pl.pallas_call(
        functools.partial(kernel, al_size, row_size),
        out_shape=jax.ShapeDtypeStruct(shape, F32),
        in_specs=[hbm, hbm, smem, smem, hbm, hbm],
        out_specs=vmem,
        scratch_shapes=[
            pltpu.VMEM((2,) + shape, F32),
            pltpu.VMEM((2, CHAINS, ROWS, R2), BF16),
            pltpu.VMEM((P_SIZE,) + plane, F32),
            pltpu.VMEM(shape, F32),
            pltpu.VMEM(shape, F32),
            pltpu.VMEM((R2, R2), BF16),
            pltpu.VMEM((ROWS, ROWS), BF16),
            pltpu.VMEM((2 * SUB, ROWS), BF16),
            pltpu.VMEM((2, MIXROWS, MIXROWS), BF16),
            pltpu.VMEM(plane, F32),
            pltpu.VMEM((P_SIZE, R2), F32),
            pltpu.VMEM((P_SIZE, R2), F32),
            pltpu.VMEM((2, 2) + plane, F32),
            pltpu.VMEM((ORDER, 2, CHAINS, SUB, R2), F32),
            pltpu.VMEM((ORDER, 2, CHAINS, SUB, R2), F32),
            pltpu.VMEM((2, CHAINS, SUB, R2), F32),
            pltpu.VMEM((2, CHAINS, SUB, R2), F32),
            pltpu.VMEM((2, CHAINS, SUB, R2), F32),
            pltpu.VMEM((8, 128), jnp.int32),
            pltpu.VMEM((QUAD - 1, 8, 128), jnp.int32),
            pltpu.VMEM((8, 128), jnp.int32),
            pltpu.VMEM((quads - 1, 8, 128), jnp.int32),
            pltpu.VMEM((L2, L2), jnp.int32),
            pltpu.VMEM((P_SIZE, P_SIZE), BF16),
            pltpu.VMEM((CHUNKS - DIRECT, 2, CHUNK) + plane, F32),
            pltpu.VMEM((DIRECT, 2, CHUNK) + plane, F32),
            dma((5,)),
            dma((2, CHUNKS)),
            dma((2, CHUNKS)),
            dma((ORDER, 2, CHAINS)),
            dma((ORDER, 2, CHAINS)),
            dma((2,)),
            dma((2,)),
            dma((QUAD + quads - 2,)),
            dma((QUAD + quads - 2,)),
            dma((CHUNKS - DIRECT,)),
            dma((CHUNKS - DIRECT,)),
            dma((DIRECT,)),
            dma((DIRECT,)),
            pltpu.SemaphoreType.REGULAR,
            pltpu.SemaphoreType.REGULAR,
            pltpu.SemaphoreType.REGULAR,
        ],
        compiler_params=pltpu.CompilerParams(
            collective_id=0, has_side_effects=True, vmem_limit_bytes=48 * 1024 * 1024
        ),
    )(
        in_hbm(psi.reshape(shape)),
        in_hbm(angular),
        widths,
        field,
        in_hbm(elem_matrix),
        in_hbm(outer_matrix),
    )
    return advanced.reshape(psi.shape)


def solution(mesh):
    placed = (P("al", None, "row", None, None), P(), P("row"), P(), P(), P())
    return jax.shard_map(
        functools.partial(local, mesh.shape["al"], mesh.shape["row"]),
        mesh=mesh,
        in_specs=placed,
        out_specs=P("al", None, "row", None, None),
        check_vma=False,
    )
```

time: 88.6 us -> 70.1 us (0.79)
  the two profiles are of different devices: /device:TPU:15 before, /device:TPU:7 now
where the time goes in v3:
time: 70.1 us; the launch traced here: 70 us
  Pallas kernels  67.3 us (96%)
  local copies, waits for them, and re-layouts  1.32 us (2%)
  between operations  1.3 us (2%)
    pallas_call x1, Pallas kernels, local(): pl.pallas_call(functools.partial(kernel, al_size, row_size), out_shape=ja...  67.3 us

profile of v3, /device:TPU:7, one launch (start us, length us, event | category | flops | bytes accessed | tf_op | source)
XLA Modules:
  0.0 70.0 jit_solution(15479562787775529218)
XLA Ops:
  1.3 67.3 %shard_map.64 = f32[2,32,2,8,512]{4,3,2,1,0:T(8,128)S(1)} custom-call(f32[2,32,2,8,512]{4,3,2,1,0:T(8,128)} %bitcast.3, s32[16,16]{1,0:T(8,128)} %ang_hbm.1, s32[1]{0:T(128)S(6)} %copy.8.widths, f32[1]{0:T(128)S(6)} %copy.9.field, bf16[32,32]{1,0:T(8,128)(2,1)} %elem_hbm.1, bf16[512,512]{1,0:T(8,128)(2,1)} %outer_hbm.1), custom_call_target="tpu_custom_call" | custom-call | tf_op jit(solution)/shard_map/pallas_call | solution.py:655
  68.6 1.3 %copy.10 = f32[1,2,32,16,512]{4,3,2,1,0:T(8,128)} copy(f32[1,2,32,16,512]{4,3,2,1,0:T(8,128)S(1)} %bitcast.2) | data formatting | bytes 4194304

commit v4 on v2

--- a/solution.py
+++ b/solution.py
@@ -21,11 +21,12 @@
 QUAD = 4
 CHUNKS = 16
 CHUNK = P_SIZE // CHUNKS
-DIRECT = CHUNKS // 2
+DIRECT = 8
+AHEAD = (0, 2, 3, 5, 8)
+PASSED = (8, 9, 11, 13, 16)
 MIXPLANES = 8
 MIXROWS = MIXPLANES * L2
 X_SIZE = 4
-PACE = 2
 
 dt_step = 0.35
 radius_zero = 8.0
@@ -72,7 +73,7 @@
     xs, xbs, pot, below, above, outer_m, ke, kp, mix, cent2, potn, reach,
     psi_rim, rim_in, rim_out, op, partial, w_own, w_quad, w_total, w_ys, ang, elem, held,
     local_sem, bulk_send, bulk_recv, rim_send, rim_recv, psi_send, psi_recv, w_send, w_recv,
-    held_recv, pass_send,
+    held_recv, pass_send, near_sem, twice_sem, row_sem,
 ):
     a = lax.axis_index("al")
     r = lax.axis_index("row")
@@ -88,14 +89,10 @@
     pass_from = a + inward * (X_SIZE - 1)
     pass_to = a + inward * X_SIZE
     pass_side = (passes & (x == X_SIZE - 1), passes & (x == 0))
-    al_peers = [
-        (has_al[0], a - 1),
-        (has_al[1], a + 1),
-        (at_end & (a >= X_SIZE), a - X_SIZE),
-        (at_end & (a < al_size - X_SIZE), a + X_SIZE),
-        (at_end, a + inward * (X_SIZE - 1)),
-    ]
     has_row = (r > 0, r < row_size - 1)
+    odd = x % 2 == 1
+    even = jnp.logical_not(odd)
+    al_peers = [(has_al[0], a - 1), (has_al[1], a + 1), (at_end, a + inward * (X_SIZE - 1))]
 
     fetch_psi = pltpu.make_async_copy(psi, xs.at[0], local_sem.at[0])
     fetch_acc = pltpu.make_async_copy(psi, out, local_sem.at[1])
@@ -113,29 +110,214 @@
     barrier = pltpu.get_barrier_semaphore()
     quad_peers = [y * QUAD + (q + j) % QUAD for j in range(1, QUAD)]
     y_peers = [((y + j) % quads) * QUAD + q for j in range(1, quads)]
-    for peer in quad_peers + y_peers:
-        pl.semaphore_signal(barrier, inc=1, device_id={"row": peer}, device_id_type=MESH)
-    for side in range(2):
-        step = 2 * side - 1
-
-        @pl.when(has_row[side])
-        def _():
-            pl.semaphore_signal(barrier, inc=1, device_id={"row": r + step}, device_id_type=MESH)
-
-    for present, peer in al_peers:
-
-        @pl.when(present)
-        def _():
-            pl.semaphore_signal(barrier, inc=1, device_id={"al": peer}, device_id_type=MESH)
+
+    def signal_al(sem):
+        for present, peer in al_peers:
+
+            @pl.when(present)
+            def _():
+                pl.semaphore_signal(sem, inc=1, device_id={"al": peer}, device_id_type=MESH)
+
+    al_count = 0
+    for present, _ in al_peers:
+        al_count = al_count + present.astype(jnp.int32)
+    row_count = QUAD - 1 + quads - 1
+    for present in has_row:
+        row_count = row_count + present.astype(jnp.int32)
+
+    @pl.when(odd)
+    def _():
+        signal_al(barrier)
 
     w_own[...] = jnp.full((8, 128), widths[0], jnp.int32)
+    ends = (0, P_SIZE - 1)
+
+    def rim_rounded(slot, c, end):
+        return xs[slot, c, ends[end]].astype(BF16).astype(F32)
+
+    def rim_copy(k, side):
+        return pltpu.make_async_remote_copy(
+            src_ref=rim_out.at[k, side],
+            dst_ref=rim_in.at[k, 1 - side],
+            send_sem=rim_send.at[k, side],
+            recv_sem=rim_recv.at[k, 1 - side],
+            device_id={"row": r + 2 * side - 1},
+            device_id_type=MESH,
+        )
+
+    def rim_arrival(k, side):
+        return pltpu.make_async_remote_copy(
+            src_ref=rim_out.at[k, 1 - side],
+            dst_ref=rim_in.at[k, side],
+            send_sem=rim_send.at[k, 1 - side],
+            recv_sem=rim_recv.at[k, side],
+            device_id={"row": r + 2 * side - 1},
+            device_id_type=MESH,
+        )
+
+    def psi_copy(side):
+        return pltpu.make_async_remote_copy(
+            src_ref=psi.at[:, ends[side]],
+            dst_ref=psi_rim.at[1 - side],
+            send_sem=psi_send.at[side],
+            recv_sem=psi_recv.at[1 - side],
+            device_id={"row": r + 2 * side - 1},
+            device_id_type=MESH,
+        )
+
+    def psi_arrival(side):
+        return pltpu.make_async_remote_copy(
+            src_ref=psi.at[:, ends[1 - side]],
+            dst_ref=psi_rim.at[side],
+            send_sem=psi_send.at[1 - side],
+            recv_sem=psi_recv.at[side],
+            device_id={"row": r + 2 * side - 1},
+            device_id_type=MESH,
+        )
+
+    def rim_sums(k, slot):
+        for c in range(2):
+            low, high = rim_rounded(slot, c, 0), rim_rounded(slot, c, 1)
+            for side in range(2):
+                part = partial[side, c * GROUPS : (c + 1) * GROUPS]
+                rim_out[k, side, c] = part + corner[side][0] * low + corner[side][1] * high
+
+    def send_rims(k):
+        for side in range(2):
+
+            @pl.when(has_row[side])
+            def _():
+                rim_copy(k, side).start()
+
+    bufs = (below, above)
+
+    def bulk_copy(side, i):
+        return pltpu.make_async_remote_copy(
+            src_ref=psi.at[:, pl.ds(i * CHUNK, CHUNK)],
+            dst_ref=bufs[1 - side].at[:, pl.ds(i * CHUNK, CHUNK)],
+            send_sem=bulk_send.at[side, i],
+            recv_sem=bulk_recv.at[1 - side, i],
+            device_id={"al": a + 2 * side - 1},
+            device_id_type=MESH,
+        )
+
+    def relay_copy(side, i):
+        ahead = (2 * side - 1) * (1 - X_SIZE)
+        return pltpu.make_async_remote_copy(
+            src_ref=psi.at[:, pl.ds(i * CHUNK, CHUNK)],
+            dst_ref=held.at[i - DIRECT],
+            send_sem=bulk_send.at[side, i],
+            recv_sem=held_recv.at[i - DIRECT],
+            device_id={"al": a + ahead},
+            device_id_type=MESH,
+        )
+
+    def pass_copy(side, i):
+        return pltpu.make_async_remote_copy(
+            src_ref=held.at[i - DIRECT],
+            dst_ref=bufs[1 - side].at[:, pl.ds(i * CHUNK, CHUNK)],
+            send_sem=pass_send.at[i - DIRECT],
+            recv_sem=bulk_recv.at[1 - side, i],
+            device_id={"al": pass_to},
+            device_id_type=MESH,
+        )
+
+    def pass_on(turn):
+        for i in range(PASSED[turn], PASSED[turn + 1]):
+
+            @pl.when(passes)
+            def _():
+                pltpu.make_async_remote_copy(
+                    src_ref=psi.at[:, pl.ds(i * CHUNK, CHUNK)],
+                    dst_ref=held.at[i - DIRECT],
+                    send_sem=bulk_send.at[0, i],
+                    recv_sem=held_recv.at[i - DIRECT],
+                    device_id={"al": pass_from},
+                    device_id_type=MESH,
+                ).wait_recv()
+
+            for side in range(2):
+
+                @pl.when(pass_side[side])
+                def _():
+                    pass_copy(side, i).start()
+
+    def start_bulk():
+        for i in range(CHUNKS):
+            for side in range(2):
+
+                @pl.when(has_al[side] & jnp.logical_not(wraps[side]))
+                def _():
+                    bulk_copy(side, i).start()
+
+                if i >= DIRECT:
+
+                    @pl.when(wraps[side])
+                    def _():
+                        relay_copy(side, i).start()
+
+    def start_direct(turn):
+        for side in range(2):
+
+            @pl.when(wraps[side])
+            def _():
+                for i in range(AHEAD[turn], AHEAD[turn + 1]):
+                    bulk_copy(side, i).start()
+
+    def bulk_arrival(side, i):
+        return pltpu.make_async_remote_copy(
+            src_ref=psi.at[:, pl.ds(i * CHUNK, CHUNK)],
+            dst_ref=bufs[side].at[:, pl.ds(i * CHUNK, CHUNK)],
+            send_sem=bulk_send.at[1 - side, i],
+            recv_sem=bulk_recv.at[side, i],
+            device_id={"al": a + 2 * side - 1},
+            device_id_type=MESH,
+        )
+
+    def width_copy(j, source, target, peer):
+        return pltpu.make_async_remote_copy(
+            src_ref=source,
+            dst_ref=target,
+            send_sem=w_send.at[j],
+            recv_sem=w_recv.at[j],
+            device_id={"row": peer},
+            device_id_type=MESH,
+        )
+
+    quad_copies = [width_copy(j, w_own, w_quad.at[j], quad_peers[j]) for j in range(QUAD - 1)]
+    y_copies = [
+        width_copy(QUAD - 1 + j, w_total, w_ys.at[j], y_peers[j]) for j in range(quads - 1)
+    ]
+
+    @pl.when(even)
+    def _():
+        pl.semaphore_wait(barrier, al_count)
+        signal_al(near_sem)
+
+    @pl.when(odd)
+    def _():
+        pl.semaphore_wait(near_sem, al_count)
+        signal_al(twice_sem)
+        for peer in quad_peers + y_peers:
+            pl.semaphore_signal(barrier, inc=1, device_id={"row": peer}, device_id_type=MESH)
+        for side in range(2):
+
+            @pl.when(has_row[side])
+            def _():
+                pl.semaphore_signal(
+                    barrier, inc=1, device_id={"row": r + 2 * side - 1}, device_id_type=MESH
+                )
+
+    start_bulk()
+
+    start_direct(0)
+
     wide = jnp.full((8, 128), widths[0], jnp.int32).astype(F32)
     scale = jnp.max(4.0 / (wide * wide))
     for fetch in fetch_small:
         fetch.wait()
     ef = elem[...].astype(F32)
     ri, ci = iota((P_SIZE, P_SIZE), 0), iota((P_SIZE, P_SIZE), 1)
-    ends = (0, P_SIZE - 1)
     corner = [[jnp.sum(jnp.where((ri == i) & (ci == k), ef, 0.0)) * scale for k in ends] for i in ends]
     wide_rows = dot(spread(ROWS, SUB, P_SIZE), elem[...]).astype(BF16)
     kron = dot(wide_rows, spread_t(ROWS, SUB, P_SIZE))
@@ -146,6 +328,49 @@
     kron = jnp.where(inside, kron, 0.0)
     kp[...] = jnp.concatenate([kron[0:SUB], kron[ROWS - SUB :]], 0).astype(BF16)
 
+    fetch_psi.wait()
+    fetch_outer.wait()
+
+    def partial_sums(slot, block):
+        sums = dot(kp[...], xbs[slot, block]) * scale
+        partial[0, block] = sums[0:SUB]
+        partial[1, block] = sums[SUB:]
+
+    def round_start(block, _):
+        c, g = block // GROUPS, block % GROUPS
+        xbs[0, block] = xs[0, c, :, g].reshape(ROWS, R2).astype(BF16)
+        partial_sums(0, block)
+        return 0
+
+    lax.fori_loop(0, 2 * GROUPS, round_start, 0)
+
+    rim_sums(0, 0)
+
+    @pl.when(odd)
+    def _():
+        pl.semaphore_wait(barrier, row_count)
+        pl.semaphore_signal(row_sem, inc=1, device_id={"al": a - 1}, device_id_type=MESH)
+
+    @pl.when(even)
+    def _():
+        pl.semaphore_wait(row_sem, 1)
+
+    for copy in quad_copies:
+        copy.start()
+    for side in range(2):
+
+        @pl.when(has_row[side])
+        def _():
+            psi_copy(side).start()
+
+    send_rims(0)
+    start_direct(1)
+
+    @pl.when(even)
+    def _():
+        pl.semaphore_wait(twice_sem, al_count)
+
+    pass_on(0)
     angf = ang[...]
     slots = iota((L2, L2), 0)
 
@@ -183,196 +408,7 @@
 
             lax.fori_loop(0, P_SIZE, clear, 0)
 
-    fetch_psi.wait()
-    fetch_outer.wait()
-
-    def partial_sums(slot, block):
-        sums = dot(kp[...], xbs[slot, block]) * scale
-        partial[0, block] = sums[0:SUB]
-        partial[1, block] = sums[SUB:]
-
-    def round_start(block, _):
-        c, g = block // GROUPS, block % GROUPS
-        xbs[0, block] = xs[0, c, :, g].reshape(ROWS, R2).astype(BF16)
-        partial_sums(0, block)
-        return 0
-
-    lax.fori_loop(0, 2 * GROUPS, round_start, 0)
-
-    def rim_rounded(slot, c, end):
-        return xs[slot, c, ends[end]].astype(BF16).astype(F32)
-
-    def rim_copy(k, side):
-        return pltpu.make_async_remote_copy(
-            src_ref=rim_out.at[k, side],
-            dst_ref=rim_in.at[k, 1 - side],
-            send_sem=rim_send.at[k, side],
-            recv_sem=rim_recv.at[k, 1 - side],
-            device_id={"row": r + 2 * side - 1},
-            device_id_type=MESH,
-        )
-
-    def rim_arrival(k, side):
-        return pltpu.make_async_remote_copy(
-            src_ref=rim_out.at[k, 1 - side],
-            dst_ref=rim_in.at[k, side],
-            send_sem=rim_send.at[k, 1 - side],
-            recv_sem=rim_recv.at[k, side],
-            device_id={"row": r + 2 * side - 1},
-            device_id_type=MESH,
-        )
-
-    def psi_copy(side):
-        return pltpu.make_async_remote_copy(
-            src_ref=psi.at[:, ends[side]],
-            dst_ref=psi_rim.at[1 - side],
-            send_sem=psi_send.at[side],
-            recv_sem=psi_recv.at[1 - side],
-            device_id={"row": r + 2 * side - 1},
-            device_id_type=MESH,
-        )
-
-    def psi_arrival(side):
-        return pltpu.make_async_remote_copy(
-            src_ref=psi.at[:, ends[1 - side]],
-            dst_ref=psi_rim.at[side],
-            send_sem=psi_send.at[1 - side],
-            recv_sem=psi_recv.at[side],
-            device_id={"row": r + 2 * side - 1},
-            device_id_type=MESH,
-        )
-
-    def rim_sums(k, slot):
-        for c in range(2):
-            low, high = rim_rounded(slot, c, 0), rim_rounded(slot, c, 1)
-            for side in range(2):
-                part = partial[side, c * GROUPS : (c + 1) * GROUPS]
-                rim_out[k, side, c] = part + corner[side][0] * low + corner[side][1] * high
-
-    def send_rims(k):
-        for side in range(2):
-
-            @pl.when(has_row[side])
-            def _():
-                rim_copy(k, side).start()
-
-    bufs = (below, above)
-
-    def bulk_copy(side, i):
-        return pltpu.make_async_remote_copy(
-            src_ref=psi.at[:, pl.ds(i * CHUNK, CHUNK)],
-            dst_ref=bufs[1 - side].at[:, pl.ds(i * CHUNK, CHUNK)],
-            send_sem=bulk_send.at[side, i],
-            recv_sem=bulk_recv.at[1 - side, i],
-            device_id={"al": a + 2 * side - 1},
-            device_id_type=MESH,
-        )
-
-    def relay_copy(side, i):
-        ahead = (2 * side - 1) * (1 - X_SIZE)
-        return pltpu.make_async_remote_copy(
-            src_ref=psi.at[:, pl.ds(i * CHUNK, CHUNK)],
-            dst_ref=held.at[i - DIRECT],
-            send_sem=bulk_send.at[side, i],
-            recv_sem=held_recv.at[i - DIRECT],
-            device_id={"al": a + ahead},
-            device_id_type=MESH,
-        )
-
-    def pass_copy(side, i):
-        return pltpu.make_async_remote_copy(
-            src_ref=held.at[i - DIRECT],
-            dst_ref=bufs[1 - side].at[:, pl.ds(i * CHUNK, CHUNK)],
-            send_sem=pass_send.at[i - DIRECT],
-            recv_sem=bulk_recv.at[1 - side, i],
-            device_id={"al": pass_to},
-            device_id_type=MESH,
-        )
-
-    def pass_on(turn):
-        for i in range(DIRECT + PACE * turn, DIRECT + PACE * (turn + 1)):
-
-            @pl.when(passes)
-            def _():
-                pltpu.make_async_remote_copy(
-                    src_ref=psi.at[:, pl.ds(i * CHUNK, CHUNK)],
-                    dst_ref=held.at[i - DIRECT],
-                    send_sem=bulk_send.at[0, i],
-                    recv_sem=held_recv.at[i - DIRECT],
-                    device_id={"al": pass_from},
-                    device_id_type=MESH,
-                ).wait_recv()
-
-            for side in range(2):
-
-                @pl.when(pass_side[side])
-                def _():
-                    pass_copy(side, i).start()
-
-    def start_bulk():
-        for side in range(2):
-
-            @pl.when(has_al[side] & jnp.logical_not(wraps[side]))
-            def _():
-                for i in range(CHUNKS):
-                    bulk_copy(side, i).start()
-
-            @pl.when(wraps[side])
-            def _():
-                for i in range(DIRECT, CHUNKS):
-                    relay_copy(side, i).start()
-
-    def start_direct(turn):
-        for side in range(2):
-
-            @pl.when(wraps[side])
-            def _():
-                for i in range(PACE * turn, PACE * (turn + 1)):
-                    bulk_copy(side, i).start()
-
-    def bulk_arrival(side, i):
-        return pltpu.make_async_remote_copy(
-            src_ref=psi.at[:, pl.ds(i * CHUNK, CHUNK)],
-            dst_ref=bufs[side].at[:, pl.ds(i * CHUNK, CHUNK)],
-            send_sem=bulk_send.at[1 - side, i],
-            recv_sem=bulk_recv.at[side, i],
-            device_id={"al": a + 2 * side - 1},
-            device_id_type=MESH,
-        )
-
-    def width_copy(j, source, target, peer):
-        return pltpu.make_async_remote_copy(
-            src_ref=source,
-            dst_ref=target,
-            send_sem=w_send.at[j],
-            recv_sem=w_recv.at[j],
-            device_id={"row": peer},
-            device_id_type=MESH,
-        )
-
-    quad_copies = [width_copy(j, w_own, w_quad.at[j], quad_peers[j]) for j in range(QUAD - 1)]
-    y_copies = [
-        width_copy(QUAD - 1 + j, w_total, w_ys.at[j], y_peers[j]) for j in range(quads - 1)
-    ]
-
-    rim_sums(0, 0)
     fetch_acc.wait()
-    degree = QUAD - 1 + quads - 1
-    for present in [present for present, _ in al_peers] + list(has_row):
-        degree = degree + present.astype(jnp.int32)
-    pl.semaphore_wait(barrier, degree)
-
-    for copy in quad_copies:
-        copy.start()
-    for side in range(2):
-
-        @pl.when(has_row[side])
-        def _():
-            psi_copy(side).start()
-
-    send_rims(0)
-    start_bulk()
-    start_direct(0)
 
     total = w_own[...]
     lower = jnp.zeros((8, 128), jnp.int32)
@@ -504,15 +540,15 @@
         psi_op.append(parts)
     finish_rims(1, 0, 1)
     for k in range(2, ORDER + 1):
-        start_direct(k - 1)
-        pass_on(k - 2)
+        if k < ORDER:
+            start_direct(k)
+        pass_on(k - 1)
         old, new = (k - 1) % 2, k % 2
         blocks_of(k, old, new)
         if k == 4:
             receive_planes(0, 8)
+            receive_planes(8, 8)
         finish_rims(k, old, new)
-    pass_on(ORDER - 1)
-    receive_planes(8, 8)
     receive_planes(16, 8)
     receive_planes(24, 4)
     receive_planes(28, 4)
@@ -588,6 +624,9 @@
             dma((QUAD + quads - 2,)),
             dma((CHUNKS - DIRECT,)),
             dma((CHUNKS - DIRECT,)),
+            pltpu.SemaphoreType.REGULAR,
+            pltpu.SemaphoreType.REGULAR,
+            pltpu.SemaphoreType.REGULAR,
         ],
         compiler_params=pltpu.CompilerParams(
             collective_id=0, has_side_effects=True, vmem_limit_bytes=48 * 1024 * 1024

time: 66.1 us -> 64.8 us (0.980)
  the two profiles are of different devices: /device:TPU:62 before, /device:TPU:78 now
where the time goes in v4:
time: 64.8 us; the launch traced here: 64.7 us
  Pallas kernels  62.1 us (96%)
  local copies, waits for them, and re-layouts  1.32 us (2%)
  between operations  1.3 us (2%)
    pallas_call x1, Pallas kernels, local(): pl.pallas_call(functools.partial(kernel, al_size, row_size), out_shape=ja...  62.1 us
    unnamed x1, local copies, waits for them, and re-layouts  1.32 us

profile of v4, /device:TPU:78, one launch (start us, length us, event | category | flops | bytes accessed | tf_op | source)
XLA Modules:
  0.0 64.7 jit_solution(234615161045187942)
XLA Ops:
  1.3 62.1 %shard_map.64 = f32[2,32,2,8,512]{4,3,2,1,0:T(8,128)S(1)} custom-call(f32[2,32,2,8,512]{4,3,2,1,0:T(8,128)} %bitcast.3, s32[16,16]{1,0:T(8,128)} %ang_hbm.1, s32[1]{0:T(128)S(6)} %copy.8.widths, f32[1]{0:T(128)S(6)} %copy.9.field, bf16[32,32]{1,0:T(8,128)(2,1)} %elem_hbm.1, bf16[512,512]{1,0:T(8,128)(2,1)} %outer_hbm.1), custom_call_target="tpu_custom_call" | custom-call | tf_op jit(solution)/shard_map/pallas_call | solution.py:586
  63.4 1.3 %copy.10 = f32[1,2,32,16,512]{4,3,2,1,0:T(8,128)} copy(f32[1,2,32,16,512]{4,3,2,1,0:T(8,128)S(1)} %bitcast.2) | data formatting | bytes 4194304

commit v5 on v4

--- a/solution.py
+++ b/solution.py
@@ -22,8 +22,8 @@
 CHUNKS = 16
 CHUNK = P_SIZE // CHUNKS
 DIRECT = 8
-AHEAD = (0, 2, 3, 5, 8)
-PASSED = (8, 9, 11, 13, 16)
+AHEAD = (0, 2, 2, 4, 8)
+PASSED = (8, 8, 10, 12, 16)
 MIXPLANES = 8
 MIXROWS = MIXPLANES * L2
 X_SIZE = 4

time: 64.8 us -> 67.6 us (1.043)
  Pallas kernels: 62.1 us -> 64.8 us
    pallas_call x1, Pallas kernels: 62.1 us -> 64.8 us  [local(): pl.pallas_call(functools.partial(kernel, al_size, row_size), out_shape=ja...]
where the time goes in v5:
time: 67.6 us; the launch traced here: 67.4 us
  Pallas kernels  64.8 us (96%)
  local copies, waits for them, and re-layouts  1.32 us (2%)
  between operations  1.3 us (2%)
    pallas_call x1, Pallas kernels, local(): pl.pallas_call(functools.partial(kernel, al_size, row_size), out_shape=ja...  64.8 us

profile of v5, /device:TPU:78, one launch (start us, length us, event | category | flops | bytes accessed | tf_op | source)
XLA Modules:
  0.0 67.4 jit_solution(9087968215706722076)
XLA Ops:
  1.3 64.8 %shard_map.64 = f32[2,32,2,8,512]{4,3,2,1,0:T(8,128)S(1)} custom-call(f32[2,32,2,8,512]{4,3,2,1,0:T(8,128)} %bitcast.3, s32[16,16]{1,0:T(8,128)} %ang_hbm.1, s32[1]{0:T(128)S(6)} %copy.8.widths, f32[1]{0:T(128)S(6)} %copy.9.field, bf16[32,32]{1,0:T(8,128)(2,1)} %elem_hbm.1, bf16[512,512]{1,0:T(8,128)(2,1)} %outer_hbm.1), custom_call_target="tpu_custom_call" | custom-call | tf_op jit(solution)/shard_map/pallas_call | solution.py:586
  66.1 1.3 %copy.10 = f32[1,2,32,16,512]{4,3,2,1,0:T(8,128)} copy(f32[1,2,32,16,512]{4,3,2,1,0:T(8,128)S(1)} %bitcast.2) | data formatting | bytes 4194304
